TPU v7x, 32 devices: a whole 2x2x4 slice. The times are simulated.
32 devices in a mesh: leaf: 32 (over z, y, x, core).
Axes of the slice: x: 2, y: 2, z: 4, core: 2. Of those that a mesh axis runs over, the one named last changes fastest.
Arguments:
- vectors: float32 [16, 131072], P(None, 'leaf'), may hold values from -6 to 6
- morton_order: int32 [32, 4096], P('leaf'), may hold values from 0 to 4095, each once within a row
- leaf_sizes: int32 [32, 32], P('leaf'), may hold values from 1 to 256, 4096 in all within a row
- leaf_basis: bfloat16 [32, 131072], P(None, 'leaf'), may hold values from -0.5 to 0.5
- leaf_transfer: bfloat16 [1024, 1024], P('leaf'), may hold values from -0.75 to 0.75
- mid_transfer: bfloat16 [128, 1024], P('leaf'), may hold values from -1 to 1
- root_transfer: bfloat16 [32, 1024], P('leaf'), may hold values from -0.75 to 0.75
- leaf_pairs: int32 [2, 2048], P(None, 'leaf'), may hold values from 0 to 31, as said below
- leaf_coupling: bfloat16 [2048, 1024], P('leaf'), may hold values from -0.5 to 0.5
- dev_partner: int32 [32, 16], P('leaf'), may hold values from -1 to 31, as said below
- dev_coupling: bfloat16 [512, 1024], P('leaf'), may hold values from -0.25 to 0.25
- grp_partner: int32 [32, 4], P('leaf'), may hold values from 0 to 3, as said below
- grp_coupling: bfloat16 [128, 1024], P('leaf'), may hold values from -0.5 to 0.5
Outputs:
- far_field: float32 [16, 131072], P(None, 'leaf')
Inputs may be any that keep to these rules, and one draw needn't show every extreme that they name: `morton_order`: each row is a permutation of 0 to 4095. `leaf_pairs`: the two leaves of a pair differ. `dev_partner`: live entries of a row come first, are distinct and never the row's own subtree; an unordered pair of subtrees appears in at most one slot of all rows; some row has all 16 slots live. `grp_partner`: never the device's own group.
All inputs are finite; a program needn't handle non-finite values.
Results may differ from a plain program's by a relative error of at most 0.014.
Values may be sent and summed in bfloat16 or wider, within the bound.
No kernel may reach another device: no remote copies, remote signals or barrier semaphores. Data moves between devices by JAX's collectives and lax.ppermute only.
A program may use at most 64 MiB of HBM per device.

v0:
```python
import jax
import jax.numpy as jnp
from jax import lax
from jax.sharding import PartitionSpec as P

LEAF = 256


highest = lax.Precision.HIGHEST


def windows(sizes, total):
    starts = jnp.cumsum(sizes) - sizes
    offset = jnp.arange(LEAF, dtype=jnp.int32)
    places = starts[:, None] + offset[None, :]
    inside = offset[None, :] < sizes[:, None]
    return (jnp.minimum(places, total - 1), inside)


def body(
    vectors,
    morton_order,
    leaf_sizes,
    leaf_basis,
    leaf_transfer,
    mid_transfer,
    root_transfer,
    leaf_pairs,
    leaf_coupling,
    dev_partner,
    dev_coupling,
    grp_partner,
    grp_coupling,
):
    basis_rank = leaf_basis.shape[0]
    count_vec = vectors.shape[0]
    points = vectors.shape[1]
    leaves = leaf_sizes.shape[1]
    middle = mid_transfer.shape[0]
    row_width = basis_rank * count_vec
    subtrees = lax.axis_size("leaf")
    groups = subtrees // 8
    self_id = lax.axis_index("leaf")
    own_group = self_id // 8
    morton = morton_order[0]
    places, inside = windows(leaf_sizes[0], points)
    sorted_vec = vectors[:, morton].astype(jnp.bfloat16)
    basis_win = leaf_basis[:, places]
    vec_win = jnp.where(inside[None], sorted_vec[:, places], jnp.zeros((), jnp.bfloat16))
    leaf_coeff = jnp.einsum(
        "rls,vls->lrv", basis_win, vec_win, preferred_element_type=jnp.float32
    ).astype(jnp.bfloat16)
    leaf_maps = leaf_transfer.reshape(leaves, basis_rank, basis_rank)
    mid_maps = mid_transfer.reshape(middle, basis_rank, basis_rank)
    root_map = root_transfer.reshape(basis_rank, basis_rank)
    child = jnp.einsum("lij,liv->ljv", leaf_maps, leaf_coeff, preferred_element_type=jnp.float32)
    mid_coeff = child.reshape(middle, 8, basis_rank, count_vec).sum(1).astype(jnp.bfloat16)
    root_coeff = jnp.einsum(
        "mij,miv->jv", mid_maps, mid_coeff, preferred_element_type=jnp.float32
    ).astype(jnp.bfloat16)
    group_term = jnp.einsum(
        "ij,iv->jv", root_map, root_coeff, preferred_element_type=jnp.float32
    ).astype(jnp.bfloat16)
    dev_blocks = dev_coupling.reshape(-1, basis_rank, basis_rank)
    partner = dev_partner[0]
    is_live = partner >= 0
    sent_back = jnp.einsum(
        "cij,iv->cjv", dev_blocks, root_coeff, preferred_element_type=jnp.float32
    ).reshape(-1, row_width)
    sent_back = jnp.where(is_live[:, None], sent_back, 0.0)
    every = jnp.arange(subtrees, dtype=jnp.int32)
    own_flat = root_coeff.reshape(1, row_width)
    term_flat = group_term.reshape(1, row_width)
    coeff_all, term_all = (
        lax.all_gather(own_flat, "leaf", axis=0, tiled=True),
        lax.all_gather(term_flat, "leaf", axis=0, tiled=True),
    )
    row_count = coeff_all.shape[0]
    here_ids = jnp.arange(row_count, dtype=jnp.int32)
    picker = (partner[:, None] == here_ids[None, :]).astype(jnp.bfloat16)
    chosen = jnp.dot(picker, coeff_all, preferred_element_type=jnp.float32).astype(jnp.bfloat16)
    chosen = chosen.reshape(-1, basis_rank, count_vec)
    near_sum = jnp.einsum("cij,cjv->iv", dev_blocks, chosen, preferred_element_type=jnp.float32)
    member = ((here_ids // 8)[None, :] == jnp.arange(groups, dtype=jnp.int32)[:, None]).astype(
        jnp.bfloat16
    )
    group_sum = jnp.dot(member, term_all, preferred_element_type=jnp.float32)
    near_sum, group_sum = (near_sum, group_sum)
    group_coeff = group_sum.astype(jnp.bfloat16)
    grp_blocks = grp_coupling.reshape(-1, basis_rank, basis_rank)
    group_hot = (grp_partner[0][:, None] == jnp.arange(groups, dtype=jnp.int32)[None, :]).astype(
        jnp.bfloat16
    )
    far_coeff = jnp.dot(group_hot, group_coeff, preferred_element_type=jnp.float32).astype(
        jnp.bfloat16
    )
    far_coeff = far_coeff.reshape(-1, basis_rank, count_vec)
    home_coeff = lax.dynamic_slice_in_dim(group_coeff, own_group, 1, 0).reshape(
        basis_rank, count_vec
    )
    to_own = jnp.einsum(
        "cij,cjv->iv", grp_blocks, far_coeff, preferred_element_type=jnp.float32
    ).reshape(1, row_width)
    to_far = jnp.einsum(
        "cij,iv->cjv", grp_blocks, home_coeff, preferred_element_type=jnp.float32
    ).reshape(-1, row_width)
    self_hot = (jnp.arange(groups, dtype=jnp.int32) == own_group).astype(jnp.float32)[:, None]
    group_rows = self_hot * to_own + jnp.dot(
        group_hot.astype(jnp.float32).T, to_far, precision=highest
    )
    partner_hot = (partner[:, None] == every[None, :]).astype(jnp.float32)
    dev_buffer = jnp.dot(partner_hot.T, sent_back, precision=highest)
    dev_back = lax.psum_scatter(dev_buffer, "leaf", scatter_dimension=0, tiled=True)
    group_total = lax.psum(group_rows, "leaf")
    group_here = lax.dynamic_slice_in_dim(group_total, own_group, 1, 0)
    root_far = near_sum + dev_back.reshape(basis_rank, count_vec)
    group_far = group_here.reshape(basis_rank, count_vec).astype(jnp.bfloat16)
    from_group = jnp.dot(root_map, group_far, preferred_element_type=jnp.float32)
    root_total = (root_far + from_group).astype(jnp.bfloat16)
    mid_total = jnp.einsum(
        "mij,jv->miv", mid_maps, root_total, preferred_element_type=jnp.float32
    ).astype(jnp.bfloat16)
    leaf_blocks = leaf_coupling.reshape(-1, basis_rank, basis_rank)
    leaf_ids = jnp.arange(leaves, dtype=jnp.int32)
    first_hot = (leaf_pairs[0][:, None] == leaf_ids[None, :]).astype(jnp.bfloat16)
    second_hot = (leaf_pairs[1][:, None] == leaf_ids[None, :]).astype(jnp.bfloat16)
    flat_coeff = leaf_coeff.reshape(leaves, row_width)
    from_second = jnp.dot(second_hot, flat_coeff, preferred_element_type=jnp.float32).astype(
        jnp.bfloat16
    )
    from_first = jnp.dot(first_hot, flat_coeff, preferred_element_type=jnp.float32).astype(
        jnp.bfloat16
    )
    forward = jnp.einsum(
        "pij,pjv->piv",
        leaf_blocks,
        from_second.reshape(-1, basis_rank, count_vec),
        preferred_element_type=jnp.float32,
    )
    backward = jnp.einsum(
        "pij,piv->pjv",
        leaf_blocks,
        from_first.reshape(-1, basis_rank, count_vec),
        preferred_element_type=jnp.float32,
    )
    leaf_far = jnp.dot(
        first_hot.astype(jnp.float32).T, forward.reshape(-1, row_width), precision=highest
    )
    leaf_far = leaf_far + jnp.dot(
        second_hot.astype(jnp.float32).T, backward.reshape(-1, row_width), precision=highest
    )
    parent = jnp.repeat(mid_total, 8, axis=0)
    leaf_down = jnp.einsum("lij,ljv->liv", leaf_maps, parent, preferred_element_type=jnp.float32)
    leaf_total = (leaf_down + leaf_far.reshape(leaves, basis_rank, count_vec)).astype(jnp.bfloat16)
    out_win = jnp.einsum("rls,lrv->vls", basis_win, leaf_total, preferred_element_type=jnp.float32)
    out_win = jnp.where(inside[None], out_win, 0.0)
    sorted_out = jnp.zeros((count_vec, points), jnp.float32).at[:, places].add(out_win)
    return jnp.zeros((count_vec, points), jnp.float32).at[:, morton].set(sorted_out)


def solution(mesh):
    in_specs = (
        P(None, "leaf"),
        P("leaf", None),
        P("leaf", None),
        P(None, "leaf"),
        P("leaf", None),
        P("leaf", None),
        P("leaf", None),
        P(None, "leaf"),
        P("leaf", None),
        P("leaf", None),
        P("leaf", None),
        P("leaf", None),
        P("leaf", None),
    )
    out_specs = P(None, "leaf")
    return jax.shard_map(body, mesh=mesh, in_specs=in_specs, out_specs=out_specs, check_vma=False)
```

profile of v0, /device:TPU:1, one launch (start us, length us, event | category | flops | bytes accessed | tf_op | source)
XLA Modules:
  0.0 286.4 jit_solution(9776952811898141529)
XLA Ops:
  6.5 1.2 broadcast_compare_fusion
  7.7 1.3 iota_compare_fusion.4
  9.1 0.7 compare_select_fusion
  9.8 0.7 copy.55
  12.7 1.4 reshape.223
  14.1 0.9 reshape.226
  15.0 1.1 reshape.221
  16.1 1.4 copy.58
  17.5 12.1 %gather_fusion.1 = bf16[4096,16]{1,0:T(8,128)(2,1)S(1)} fusion(bf16[16,4096]{0,1:T(8,128)(2,1)S(1)} %copy.58, s32[4096]{0:T(1024)S(1)} %broadcast_clamp_fusion.1), kind=kCustom, calls=%fused_computation.1 | custom fusion | bytes 278528 | tf_op jit(solution)/shard_map/gather | solution.py:47
  29.7 27.9 %gather_fusion.2 = bf16[8192,16]{1,0:T(8,128)(2,1)S(1)} fusion(bf16[16,4096]{0,1:T(8,128)(2,1)S(1)} %bitcast.137, s32[8192]{0:T(1024)} %broadcast_clamp_fusion), kind=kCustom, calls=%fused_computation.2 | custom fusion | bytes 557056 | tf_op jit(solution)/shard_map/gather | solution.py:49
  57.6 1.4 copy.59
  59.1 1.4 copy.56
  60.5 27.9 %gather_fusion = bf16[8192,32]{1,0:T(8,128)(2,1)S(1)} fusion(bf16[32,4096]{0,1:T(8,128)(2,1)S(1)} %copy.56, s32[8192]{0:T(1024)} %broadcast_clamp_fusion), kind=kCustom, calls=%fused_computation | custom fusion | bytes 1081344 | tf_op jit(solution)/shard_map/gather | solution.py:48
  88.5 0.8 copy.57
  90.6 0.9 fusion.28
  92.2 0.8 copy.73
  93.4 43.3 %all-gather = bf16[32,1,512]{2,1,0:T(2,128)(2,1)S(1)} all-gather(bf16[1,1,512]{2,1,0:T(2,128)(2,1)S(1)} %reshape.286), channel_id=1, replica_groups=mesh['leaf'=32] {'leaf'}, dimensions={0}, use_global_device_ids=true | all-gather | bytes 33792 | tf_op jit(solution)/shard_map/all_gather | solution.py:75
  136.9 36.8 %all-gather.1 = bf16[32,1,512]{2,1,0:T(2,128)(2,1)S(1)} all-gather(bf16[1,1,512]{2,1,0:T(2,128)(2,1)S(1)} %reshape.288), channel_id=1, replica_groups=mesh['leaf'=32] {'leaf'}, dimensions={0}, use_global_device_ids=true | all-gather | bytes 33792 | tf_op jit(solution)/shard_map/all_gather | solution.py:76
  178.4 35.6 %psum.7 = bf16[4,512]{1,0:T(4,128)(2,1)S(1)} all-reduce(f32[4,512]{1,0:T(4,128)S(1)} %convolution_add_fusion.1), channel_id=1, replica_groups=mesh['leaf'=32] {'leaf'}, use_global_device_ids=true, to_apply=%region_3.4 | all-reduce | flops 2048 | bytes 12288 | tf_op jit(solution)/shard_map/psum | solution.py:114
  215.2 0.7 dynamic-slice_reduce_fusion
  217.0 2.6 copy.88
  219.6 45.0 %scatter_custom_fusion = f32[16,4096]{0,1:T(8,128)S(1)} fusion(s32[8192]{0:T(1024)} %bitcast.151, f32[8192,16]{1,0:T(8,128)} %bitcast.138, f32[]{:T(128)} %constant.39.clone.1), kind=kCustom, calls=%fused_computation.39 | custom fusion | flops 131072 | bytes 262656 | tf_op jit(solution)/shard_map/scatter-add | solution.py:157
  264.6 12.1 %scatter_custom_fusion.1 = f32[16,4096]{0,1:T(8,128)} fusion(s32[4096]{0:T(1024)S(1)} %bitcast.154, f32[16,4096]{0,1:T(8,128)S(1)} %scatter_custom_fusion, f32[]{:T(128)} %constant.39.clone.1), kind=kCustom, calls=%fused_computation.5 | custom fusion | bytes 2359300 | tf_op jit(solution)/shard_map/scatter | solution.py:158
  276.6 2.9 %copy.83 = f32[16,4096]{1,0:T(8,128)} copy(f32[16,4096]{0,1:T(8,128)} %scatter_custom_fusion.1) | data formatting | bytes 524288 | tf_op jit(solution)/shard_map/scatter | solution.py:158
  (91 shorter events, 11.4 us)
Async XLA Ops:
  6.5 208.7 %all-reduce.3.cloned.1.call-start = ((), (), s32[]{:S(2)}) async-start(), calls=%async_computation | async-start | bytes 131072
  11.5 0.6 copy-start.4
  88.4 1.0 copy-start.2
  88.4 0.9 copy-start.5
  88.5 1.5 copy-start
  89.4 1.2 copy-start.10
  89.4 1.2 copy-start.12
  89.4 2.4 copy-start.9
  89.4 2.4 copy-start.8
  89.4 2.5 copy-start.7
  89.4 2.6 copy-start.3
  89.4 84.4 %copy-start.11 = (s32[1,4]{1,0:T(1,128)S(1)}, s32[1,4]{1,0:T(1,128)}, u32[]{:S(2)}) copy-start(s32[1,4]{1,0:T(1,128)} %param.24) | copy-start | bytes 52
  176.9 39.5 %copy-start.1 = (bf16[4,32,32]{2,1,0:T(8,128)(2,1)S(1)}, bf16[4,32,32]{2,1,0:T(8,128)(2,1)}, u32[]{:S(2)}) copy-start(bf16[4,32,32]{2,1,0:T(8,128)(2,1)} %reshape.223) | copy-start | bytes 24580
  176.9 39.8 %copy-start.6 = (pred[32,256]{1,0:T(8,128)(4,1)S(1)}, pred[32,256]{1,0:T(8,128)(4,1)}, u32[]{:S(2)}) copy-start(pred[32,256]{1,0:T(8,128)(4,1)} %iota_compare_fusion.4) | copy-start | bytes 24580
Sparse Core Ops, SparseCore 0:
  91.6 123.5 all-reduce.2
where the time goes:
time: 290 us; the launch traced here: 286 us
  blocking collectives  116 us (40%)
  local copies, waits for them, and re-layouts  101 us (35%)
  other arithmetic  49.8 us (17%)
  between operations  13.8 us (5%)
  matrix products  5.5 us (2%)
    scatter-add x1, other arithmetic, body(): jnp.zeros((count_vec, points), jnp.float32).at[:, places].add(out_win)  45 us
    all_gather x1, blocking collectives, body(): lax.all_gather(own_flat, 'leaf', axis=0, tiled=True)  43.3 us
    all_gather x1, blocking collectives, body(): lax.all_gather(term_flat, 'leaf', axis=0, tiled=True)  36.8 us
    psum x1, blocking collectives, body(): group_total = lax.psum(group_rows, 'leaf')  35.6 us
    gather x2, local copies, waits for them, and re-layouts, body(): sorted_vec[:, places]  29.4 us
    gather x2, local copies, waits for them, and re-layouts, body(): basis_win = leaf_basis[:, places]  28.7 us
    scatter x2, local copies, waits for them, and re-layouts, body(): jnp.zeros((count_vec, points), jnp.float32).at[:, morton].set(sorted_out)  15 us
    gather x1, local copies, waits for them, and re-layouts, body(): sorted_vec = vectors[:, morton].astype(jnp.bfloat16)  12.1 us
  transfers between devices with their start and end apart: 1, of which 1 were waited for; matrix products, arithmetic and copies ran while one was open for 3% of the time, Pallas kernels for 0%

commit v1 on v0

v1 whole, which is shorter than its diff:
```python
import functools

import jax
import jax.numpy as jnp
from jax import lax
from jax.experimental import pallas as pl
from jax.experimental.pallas import tpu as pltpu
from jax.sharding import PartitionSpec as P

LEAF = 256
SPLIT = 256

bf16 = jnp.bfloat16
f32 = jnp.float32
highest = lax.Precision.HIGHEST


def dot(a, b, over):
    return lax.dot_general(a, b, (over, ((), ())), preferred_element_type=f32)


NN = ((1,), (0,))
NT = ((1,), (1,))
TN = ((0,), (0,))


def one_hot_low(morton, width):
    rows = lax.broadcasted_iota(jnp.int32, (SPLIT, width), 0)
    return jnp.where(rows == (morton & (SPLIT - 1)), 1.0, 0.0).astype(bf16)


def window(start, points, width):
    base = jnp.minimum(start // 128 * 128, points - width)
    return pl.multiple_of(base, 128)


def spread(ref, rank):
    flat = ref[...]
    return jnp.concatenate([flat[:, rank * i : rank * (i + 1)] for i in range(rank)], axis=0)


def spread_into(scr, ref, row, pitch, rank):
    flat = ref[...].astype(f32)
    n = flat.shape[0]
    for i in range(rank):
        scr[i * pitch + row : i * pitch + row + n, :rank] = flat[:, rank * i : rank * (i + 1)]


def up_leaf_kernel(sizes, vec_ref, morton_ref, basis_ref, coeff_ref, sorted_ref, scr):
    vecs, points = vec_ref.shape
    rank = basis_ref.shape[0]
    leaves = sizes.shape[1]
    highs = points // SPLIT
    width = min(points, LEAF + 128)
    stacked = jnp.concatenate(
        [vec_ref[:, h * SPLIT : (h + 1) * SPLIT].astype(bf16) for h in range(highs)], axis=0
    )
    step = 256
    for k in range(points // step):
        morton = morton_ref[:, k * step : (k + 1) * step]
        mixed = dot(stacked, one_hot_low(morton, step), NN)
        high = morton // SPLIT
        picked = jnp.zeros((vecs, step), f32)
        for h in range(highs):
            picked = picked + jnp.where(high == h, mixed[h * vecs : (h + 1) * vecs], 0.0)
        sorted_ref[:, k * step : (k + 1) * step] = picked
    start = jnp.int32(0)
    for l in range(leaves):
        size = sizes[0, l]
        base = window(start, points, width)
        place = base + lax.broadcasted_iota(jnp.int32, (1, width), 1)
        inside = (place >= start) & (place < start + size)
        vec = jnp.where(inside, sorted_ref[:, pl.ds(base, width)], 0.0).astype(bf16)
        scr[pl.ds(l, rank, stride=leaves), :] = dot(basis_ref[:, pl.ds(base, width)], vec, NT)
        start = start + size
    coeff_ref[...] = scr[...].astype(bf16)


def up_root_kernel(
    self_id, partner, coeff_ref, leaf_ref, mid_ref, root_ref, dev_ref, group_ref, msg_ref, scr, dev_scr
):
    rank = 32
    vecs = coeff_ref.shape[1]
    leaves = leaf_ref.shape[0]
    middle = mid_ref.shape[0]
    slots = dev_ref.shape[0]
    subtrees = msg_ref.shape[0]
    groups = group_ref.shape[0]
    lanes = middle * vecs
    maps = spread(leaf_ref, rank)
    coeff = jnp.concatenate([coeff_ref[...].astype(f32)] * middle, axis=1)
    rows = lax.broadcasted_iota(jnp.int32, (rank * leaves, lanes), 0)
    cols = lax.broadcasted_iota(jnp.int32, (rank * leaves, lanes), 1)
    mine = (rows % leaves) // 8 == cols // vecs
    coeff = jnp.where(mine, coeff, 0.0).astype(bf16)
    mid = dot(coeff, maps, TN).astype(bf16)
    spread_into(scr, mid_ref, 0, 8, rank)
    spread_into(scr, root_ref, middle, 8, rank)
    spread_into(dev_scr, dev_ref, 0, slots, rank)
    root = jnp.zeros((vecs, rank), f32)
    for m in range(middle):
        block = scr[pl.ds(m, rank, stride=8), :][:, :rank].astype(bf16)
        root = root + dot(mid[m * vecs : (m + 1) * vecs], block, NN)
    root = root.astype(bf16)
    term = dot(root, scr[pl.ds(middle, rank, stride=8), :][:, :rank].astype(bf16), NN)
    blank = jnp.zeros((vecs, rank), f32)
    for g in range(groups):
        chunk = group_ref[g : g + 1, :]
        part = jnp.concatenate(
            [chunk[:, h * rank : (h + 1) * rank] for h in range(4)]
            + [jnp.zeros((vecs - 4, rank), f32)],
            axis=0,
        )
        tile = jnp.concatenate([root.astype(f32), term, blank, part], axis=1).astype(bf16)
        for d in range(8):
            msg_ref[g * 8 + d] = tile
    for c in range(slots):
        who = partner[0, c]
        live = who >= 0
        where = jnp.where(live, who, self_id[0])
        block = dev_scr[pl.ds(c, rank, stride=slots), :][:, :rank].astype(bf16)
        back = dot(root, block, NN)
        back = jnp.where(live, back, 0.0).astype(bf16)
        msg_ref[where, :, 2 * rank : 3 * rank] = back


def down_kernel(
    sizes,
    partner,
    got_ref,
    morton_ref,
    basis_ref,
    leaf_ref,
    mid_ref,
    root_ref,
    dev_ref,
    near_ref,
    out_ref,
    got,
    scr,
    dev_scr,
    total_scr,
    sorted_ref,
):
    rank, points = basis_ref.shape
    subtrees, vecs, tile_lanes = got_ref.shape
    leaves = leaf_ref.shape[0]
    middle = mid_ref.shape[0]
    slots = dev_ref.shape[0]
    groups = subtrees // 8
    highs = points // SPLIT
    width = min(points, LEAF + 128)
    got[...] = got_ref[...].astype(f32).reshape(subtrees * vecs, tile_lanes)
    spread_into(scr, mid_ref, 0, 8, rank)
    spread_into(scr, root_ref, middle, 8, rank)
    spread_into(dev_scr, dev_ref, 0, slots, rank)
    back = jnp.zeros((vecs, rank), f32)
    far = jnp.zeros((vecs, rank), f32)
    for g in range(groups):
        total = got[g * 8 * vecs : (g * 8 + 1) * vecs, :]
        for d in range(1, 8):
            total = total + got[(g * 8 + d) * vecs : (g * 8 + d + 1) * vecs, :]
        back = back + total[:, 2 * rank : 3 * rank]
        group = total[:, rank : 2 * rank].astype(bf16)
        pitch = groups // 4
        block = got[pl.ds(g // 4 * vecs + g % 4, rank, stride=pitch * vecs), :]
        far = far + dot(group, block[:, 3 * rank : 4 * rank].astype(bf16), NT)
    total = back
    for c in range(slots):
        who = partner[0, c]
        live = who >= 0
        other = got_ref[jnp.maximum(who, 0)][:, :rank].astype(f32)
        other = jnp.where(live, other, 0.0).astype(bf16)
        block = dev_scr[pl.ds(c, rank, stride=slots), :][:, :rank].astype(bf16)
        total = total + dot(other, block, NT)
    root_map = scr[pl.ds(middle, rank, stride=8), :][:, :rank].astype(bf16)
    total = (total + dot(far.astype(bf16), root_map, NT)).astype(bf16)
    mids = []
    for m in range(middle):
        block = scr[pl.ds(m, rank, stride=8), :][:, :rank].astype(bf16)
        mids.append(dot(total, block, NT))
    mids = jnp.concatenate(mids, axis=0).astype(bf16)
    maps = spread(leaf_ref, rank)
    down = dot(maps, mids, NT)
    rows = lax.broadcasted_iota(jnp.int32, (rank * leaves, 1), 0)
    mine = (rows % leaves) // 8
    leaf = near_ref[...]
    for m in range(middle):
        leaf = leaf + jnp.where(mine == m, down[:, m * vecs : (m + 1) * vecs], 0.0)
    total_scr[...] = leaf
    start = jnp.int32(0)
    for l in range(leaves):
        size = sizes[0, l]
        base = window(start, points, width)
        place = base + lax.broadcasted_iota(jnp.int32, (1, width), 1)
        inside = (place >= start) & (place < start + size)
        leaf = total_scr[pl.ds(l, rank, stride=leaves), :].astype(bf16)
        value = dot(leaf, basis_ref[:, pl.ds(base, width)], TN)
        old = sorted_ref[:, pl.ds(base, width)]
        sorted_ref[:, pl.ds(base, width)] = jnp.where(inside, value, old)
        start = start + size
    step = 256
    result = jnp.zeros((highs * vecs, SPLIT), f32)
    for k in range(points // step):
        morton = morton_ref[:, k * step : (k + 1) * step]
        high = morton // SPLIT
        value = sorted_ref[:, k * step : (k + 1) * step]
        masked = jnp.concatenate([jnp.where(high == h, value, 0.0) for h in range(highs)], axis=0)
        result = result + dot(masked.astype(bf16), one_hot_low(morton, step), NT)
    for h in range(highs):
        out_ref[:, h * SPLIT : (h + 1) * SPLIT] = result[h * vecs : (h + 1) * vecs]


smem = pl.BlockSpec(memory_space=pltpu.SMEM)
vmem = pl.BlockSpec(memory_space=pltpu.VMEM)


def body(
    vectors,
    morton_order,
    leaf_sizes,
    leaf_basis,
    leaf_transfer,
    mid_transfer,
    root_transfer,
    leaf_pairs,
    leaf_coupling,
    dev_partner,
    dev_coupling,
    grp_partner,
    grp_coupling,
):
    rank, points = leaf_basis.shape
    vecs = vectors.shape[0]
    leaves = leaf_sizes.shape[1]
    middle = mid_transfer.shape[0]
    row_width = rank * vecs
    slots = dev_coupling.shape[0]
    subtrees = lax.axis_size("leaf")
    groups = subtrees // 8
    self_id = lax.axis_index("leaf").astype(jnp.int32)
    own_group = self_id // 8

    group_ids = jnp.arange(groups, dtype=jnp.int32)
    hot = (grp_partner[0][:, None] == group_ids[None, :]).astype(bf16)
    by_partner = jnp.einsum(
        "sh,sx->hx", hot, grp_coupling, preferred_element_type=f32
    ).reshape(groups, rank, rank)
    self_hot = (group_ids == own_group).astype(f32)
    parts = (
        self_hot[:, None, None, None] * by_partner.transpose(1, 0, 2)[None]
        + self_hot[None, None, :, None] * by_partner.transpose(0, 2, 1)[:, :, None, :]
    )
    parts = parts.astype(bf16).reshape(groups, subtrees, 4 * rank).transpose(1, 0, 2)
    chunks = lax.all_to_all(parts, "leaf", 0, 0, tiled=True)

    coeff = pl.pallas_call(
        up_leaf_kernel,
        out_shape=jax.ShapeDtypeStruct((rank * leaves, vecs), bf16),
        in_specs=[smem, vmem, vmem, vmem],
        out_specs=vmem,
        scratch_shapes=[pltpu.VMEM((vecs, points), f32), pltpu.VMEM((rank * leaves, vecs), f32)],
        name="up_leaf",
    )(leaf_sizes, vectors, morton_order, leaf_basis)

    chunk = chunks.astype(f32).sum(0)
    message = pl.pallas_call(
        up_root_kernel,
        out_shape=jax.ShapeDtypeStruct((subtrees, vecs, 4 * rank), bf16),
        in_specs=[smem, smem] + [vmem] * 6,
        out_specs=vmem,
        scratch_shapes=[
            pltpu.VMEM((rank * 8, rank), f32),
            pltpu.VMEM((rank * slots, rank), f32),
        ],
        name="up_root",
    )(
        self_id[None],
        dev_partner,
        coeff,
        leaf_transfer,
        mid_transfer,
        root_transfer,
        dev_coupling,
        chunk,
    )
    got = lax.all_to_all(message, "leaf", 0, 0, tiled=True)

    leaf_blocks = leaf_coupling.reshape(-1, rank, rank)
    leaf_ids = jnp.arange(leaves, dtype=jnp.int32)
    first_hot = (leaf_pairs[0][:, None] == leaf_ids[None, :]).astype(bf16)
    second_hot = (leaf_pairs[1][:, None] == leaf_ids[None, :]).astype(bf16)
    flat = coeff.reshape(rank, leaves, vecs).transpose(1, 0, 2).reshape(leaves, row_width)
    from_second = jnp.dot(second_hot, flat, preferred_element_type=f32).astype(bf16)
    from_first = jnp.dot(first_hot, flat, preferred_element_type=f32).astype(bf16)
    forward = jnp.einsum(
        "pij,pjv->piv", leaf_blocks, from_second.reshape(-1, rank, vecs), preferred_element_type=f32
    )
    backward = jnp.einsum(
        "pij,piv->pjv", leaf_blocks, from_first.reshape(-1, rank, vecs), preferred_element_type=f32
    )
    near = jnp.dot(first_hot.T, forward.reshape(-1, row_width).astype(bf16), preferred_element_type=f32)
    near = near + jnp.dot(
        second_hot.T, backward.reshape(-1, row_width).astype(bf16), preferred_element_type=f32
    )
    near = near.reshape(leaves, rank, vecs).transpose(1, 0, 2).reshape(rank * leaves, vecs)

    return pl.pallas_call(
        down_kernel,
        out_shape=jax.ShapeDtypeStruct((vecs, points), f32),
        in_specs=[smem, smem] + [vmem] * 8,
        out_specs=vmem,
        scratch_shapes=[
            pltpu.VMEM((subtrees * vecs, 4 * rank), f32),
            pltpu.VMEM((rank * 8, rank), f32),
            pltpu.VMEM((rank * slots, rank), f32),
            pltpu.VMEM((rank * leaves, vecs), f32),
            pltpu.VMEM((vecs, points), f32),
        ],
        name="down",
    )(
        leaf_sizes,
        dev_partner,
        got,
        morton_order,
        leaf_basis,
        leaf_transfer,
        mid_transfer,
        root_transfer,
        dev_coupling,
        near,
    )


def solution(mesh):
    in_specs = (
        P(None, "leaf"),
        P("leaf", None),
        P("leaf", None),
        P(None, "leaf"),
        P("leaf", None),
        P("leaf", None),
        P("leaf", None),
        P(None, "leaf"),
        P("leaf", None),
        P("leaf", None),
        P("leaf", None),
        P("leaf", None),
        P("leaf", None),
    )
    out_specs = P(None, "leaf")
    return jax.shard_map(body, mesh=mesh, in_specs=in_specs, out_specs=out_specs, check_vma=False)
```

time: 290 us -> 40.9 us (0.14); the launches traced: 286 us -> 40.3 us
  blocking collectives: 116 us -> 0 us
  local copies, waits for them, and re-layouts: 101 us -> 7.31 us
  other arithmetic: 49.8 us -> 1.32 us
  between operations: 13.8 us -> 0.16 us
  starting transfers between devices: 0.01 us -> 12.9 us
  Pallas kernels: 0 us -> 10.6 us
  waiting for transfers between devices: 0.55 us -> 6.2 us
  matrix products: 5.5 us -> 1.78 us
    all_gather x2 -> x0, blocking collectives: 80.1 us -> none  [the longest x1 43.3 us: body(): lax.all_gather(own_flat, 'leaf', axis=0, tiled=True)]
    gather x5 -> x0, local copies, waits for them, and re-layouts: 70.3 us -> none  [the longest x2 29.4 us: body(): sorted_vec[:, places]]
    scatter-add x1 -> x0, other arithmetic: 45 us -> none  [body(): jnp.zeros((count_vec, points), jnp.float32).at[:, places].add(out_win)]
    psum x1 -> x0, blocking collectives: 35.6 us -> none  [body(): group_total = lax.psum(group_rows, 'leaf')]
    scatter x2 -> x0, local copies, waits for them, and re-layouts: 15 us -> none  [body(): jnp.zeros((count_vec, points), jnp.float32).at[:, morton].set(sorted_out)]
    all_to_all x0 -> x2, starting transfers between devices: none -> 12.9 us  [the longest x1 7.08 us: body(): chunks = lax.all_to_all(parts, 'leaf', 0, 0, tiled=True)]
    pallas_call x0 -> x3, Pallas kernels: none -> 10.6 us  [the longest x1 4.47 us: body(): pl.pallas_call(down_kernel, out_shape=jax.ShapeDtypeStruct((vecs, points)...]
    all_to_all x0 -> x2, waiting for transfers between devices: none -> 6.2 us  [the longest x1 6.19 us: body(): got = lax.all_to_all(message, 'leaf', 0, 0, tiled=True)]
  transfers between devices with their start and end apart: 1 -> 2, of which waited for: 1 -> 1; matrix products, arithmetic and copies ran while one was open for 3% -> 15% of each run, Pallas kernels for 0% -> 9%
where the time goes in v1:
time: 40.9 us; the launch traced here: 40.3 us
  starting transfers between devices  12.9 us (32%)
  Pallas kernels  10.6 us (26%)
  local copies, waits for them, and re-layouts  7.31 us (18%)
  waiting for transfers between devices  6.2 us (15%)
  matrix products  1.78 us (4%)
  other arithmetic  1.32 us (3%)
    all_to_all x1, starting transfers between devices, body(): chunks = lax.all_to_all(parts, 'leaf', 0, 0, tiled=True)  7.08 us
    all_to_all x1, waiting for transfers between devices, body(): got = lax.all_to_all(message, 'leaf', 0, 0, tiled=True)  6.19 us
    all_to_all x1, starting transfers between devices, body(): got = lax.all_to_all(message, 'leaf', 0, 0, tiled=True)  5.83 us
    pallas_call x1, Pallas kernels, body(): pl.pallas_call(down_kernel, out_shape=jax.ShapeDtypeStruct((vecs, points)...  4.47 us
    pallas_call x1, Pallas kernels, body(): pl.pallas_call(up_leaf_kernel, out_shape=jax.ShapeDtypeStruct((rank * lea...  3.54 us
    pallas_call x1, Pallas kernels, body(): pl.pallas_call(up_root_kernel, out_shape=jax.ShapeDtypeStruct((subtrees,...  2.56 us
    unnamed x11, local copies, waits for them, and re-layouts  2.08 us
    reshape x1, local copies, waits for them, and re-layouts, body(): coeff.reshape(rank, leaves, vecs).transpose(1, 0, 2)  1.1 us
  transfers between devices with their start and end apart: 2, of which 1 were waited for; matrix products, arithmetic and copies ran while one was open for 15% of the time, Pallas kernels for 9%

profile of v1, /device:TPU:1, one launch (start us, length us, event | category | flops | bytes accessed | tf_op | source)
XLA Modules:
  0.0 40.3 jit_solution(16753619032813753657)
XLA Ops:
  0.2 0.5 %copy-done = bf16[4,1024]{1,0:T(4,128)(2,1)S(1)} copy-done((bf16[4,1024]{1,0:T(4,128)(2,1)S(1)}, bf16[4,1024]{1,0:T(4,128)(2,1)}, u32[]{:S(2)}) %copy-start) | copy-done | bytes 8216
  0.8 0.3 fusion.12
  1.6 0.7 %fusion.2 = bf16[32,4,128]{2,1,0:T(4,128)(2,1)} fusion(f32[4,32,128]{2,0,1:T(4,128)S(1)} %mul.44, f32[128]{0:T(128)S(1)} %mul.41, f32[32,128]{1,0:T(8,128)S(1)} %mul.37, f32[4]{0:T(128)S(1)} %compare_convert_fusion), kind=kLoop, calls=%fused_computation.10 | loop fusion | flops 65536 | bytes 115216 | tf_op jit(solution)/shard_map/transpose | solution.py:254
  2.3 7.1 %all-to-all-start = ((bf16[32,4,128]{2,1,0:T(4,128)(2,1)}), bf16[32,4,128]{2,1,0:T(4,128)(2,1)S(1)}, u32[]{:S(2)}, u32[]{:S(2)}) async-start(bf16[32,4,128]{2,1,0:T(4,128)(2,1)} %fusion.2), calls=%async_computation | async-start | bytes 65536 | tf_op jit(solution)/shard_map/all_to_all | solution.py:255
  9.4 3.5 %up_leaf.1.coeff_ref = bf16[1024,16]{1,0:T(8,128)(2,1)} custom-call(s32[1,32]{1,0:T(1,128)} %sizes.3, f32[16,4096]{1,0:T(8,128)} %vec_ref.1, s32[1,4096]{1,0:T(1,128)} %morton_ref.3, bf16[32,4096]{1,0:T(8,128)(2,1)} %basis_ref.3), custom_call_target="tpu_custom_call" | custom-call | tf_op jit(solution)/shard_map/up_leaf/pallas_call | solution.py:257
  13.0 1.1 %copy.34 = bf16[32,32,16]{1,2,0:T(8,128)(2,1)S(1)} copy(bf16[32,32,16]{2,1,0:T(8,128)(2,1)} %bitcast.40) | data formatting | bytes 65536 | tf_op jit(solution)/shard_map/reshape | solution.py:293
  14.4 0.3 copy.37
  14.7 0.6 %copy-done.2 = bf16[64,1024]{1,0:T(8,128)(2,1)S(1)} copy-done((bf16[64,1024]{1,0:T(8,128)(2,1)S(1)}, bf16[64,1024]{1,0:T(8,128)(2,1)}, u32[]{:S(2)}) %copy-start.2) | copy-done | bytes 131096
  15.5 0.8 %copy.38 = bf16[64,32,32]{2,1,0:T(8,128)(2,1)S(1)} copy(bf16[64,32,32]{0,2,1:T(8,128)(2,1)S(1)} %bitcast.45) | data formatting | bytes 262144 | tf_op jit(solution)/shard_map/reshape | solution.py:289
  16.3 0.2 convolution_convert_fusion.2
  16.6 0.3 copy.41
  16.9 0.4 fusion
  17.3 0.3 fusion.1
  17.6 0.3 copy.39
  18.0 0.6 %convert_reduce_fusion.group_ref = f32[4,128]{1,0:T(4,128)} fusion(bf16[32,4,128]{2,1,0:T(4,128)(2,1)S(1)} %all-to-all-done), kind=kLoop, calls=%fused_computation.8 | loop fusion | flops 32256 | bytes 34816 | tf_op jit(solution)/shard_map/reduce_sum | solution.py:266
  18.6 2.6 %up_root.1 = bf16[32,16,128]{2,1,0:T(8,128)(2,1)} custom-call(s32[1]{0:T(128)} %bitcast.self_id, s32[1,16]{1,0:T(1,128)} %partner.3, bf16[1024,16]{1,0:T(8,128)(2,1)} %up_leaf.1.coeff_ref, bf16[32,1024]{1,0:T(8,128)(2,1)} %leaf_ref.3, bf16[4,1024]{1,0:T(4,128)(2,1)} %mid_ref.3, bf16[1,1024]{1,0:T(2,128)(2,1)} %root_ref.3, bf16[16,1024]{1,0:T(8,128)(2,1)} %dev_ref.3, ...), custom_call_target="tpu_custom_call" | custom-call | tf_op jit(solution)/shard_map/up_root/pallas_call | solution.py:267
  21.1 5.8 %all-to-all-start.1 = ((bf16[32,16,128]{2,1,0:T(8,128)(2,1)}), bf16[32,16,128]{2,1,0:T(8,128)(2,1)S(1)}, u32[]{:S(2)}, u32[]{:S(2)}) async-start(bf16[32,16,128]{2,1,0:T(8,128)(2,1)} %up_root.1), calls=%async_computation.1 | async-start | bytes 262144 | tf_op jit(solution)/shard_map/all_to_all | solution.py:287
  27.0 0.2 fusion.5
  27.2 0.3 copy.43
  27.6 0.2 convolution_add_fusion
  27.9 1.0 %copy.45 = f32[32,32,16]{2,1,0:T(8,128)} copy(f32[32,32,16]{1,2,0:T(8,128)S(1)} %bitcast.44) | data formatting | bytes 131072 | tf_op jit(solution)/shard_map/transpose | solution.py:306
  29.0 6.2 %all-to-all-done.1.got_ref = bf16[32,16,128]{2,1,0:T(8,128)(2,1)S(1)} async-done(((bf16[32,16,128]{2,1,0:T(8,128)(2,1)}), bf16[32,16,128]{2,1,0:T(8,128)(2,1)S(1)}, u32[]{:S(2)}, u32[]{:S(2)}) %all-to-all-start.1) | async-done | bytes 131104 | tf_op jit(solution)/shard_map/all_to_all | solution.py:287
  35.2 0.6 %copy-done.1 = bf16[32,16,128]{2,1,0:T(8,128)(2,1)} copy-done((bf16[32,16,128]{2,1,0:T(8,128)(2,1)}, bf16[32,16,128]{2,1,0:T(8,128)(2,1)S(1)}, u32[]{:S(2)}) %copy-start.1) | copy-done | bytes 131096
  35.8 4.5 %down.1 = f32[16,4096]{1,0:T(8,128)} custom-call(s32[1,32]{1,0:T(1,128)} %sizes.3, s32[1,16]{1,0:T(1,128)} %partner.3, bf16[32,16,128]{2,1,0:T(8,128)(2,1)} %copy-done.1, s32[1,4096]{1,0:T(1,128)} %morton_ref.3, bf16[32,4096]{1,0:T(8,128)(2,1)} %basis_ref.3, bf16[32,1024]{1,0:T(8,128)(2,1)} %leaf_ref.3, bf16[4,1024]{1,0:T(4,128)(2,1)} %mid_ref.3, ...), custom_call_target="tpu_custom_call" | custom-call | tf_op jit(solution)/shard_map/down/pallas_call | solution.py:308
  (23 shorter events, 1.6 us)
Async XLA Ops:
  0.0 0.7 %copy-start = (bf16[4,1024]{1,0:T(4,128)(2,1)S(1)}, bf16[4,1024]{1,0:T(4,128)(2,1)}, u32[]{:S(2)}) copy-start(bf16[4,1024]{1,0:T(4,128)(2,1)} %param.25) | copy-start | bytes 24580
  0.2 0.7 %copy-start.4 = (s32[1,4]{1,0:T(1,128)S(1)}, s32[1,4]{1,0:T(1,128)}, u32[]{:S(2)}) copy-start(s32[1,4]{1,0:T(1,128)} %param.24) | copy-start | bytes 52
  2.3 15.6 %all-to-all-start = ((bf16[32,4,128]{2,1,0:T(4,128)(2,1)}), bf16[32,4,128]{2,1,0:T(4,128)(2,1)S(1)}, u32[]{:S(2)}, u32[]{:S(2)}) async-start(bf16[32,4,128]{2,1,0:T(4,128)(2,1)} %fusion.2), calls=%async_computation | async-start | bytes 65536 | tf_op jit(solution)/shard_map/all_to_all | solution.py:255
  13.0 1.1 %copy-start.3 = (s32[2,64]{1,0:T(2,128)S(1)}, s32[2,64]{1,0:T(2,128)}, u32[]{:S(2)}) copy-start(s32[2,64]{1,0:T(2,128)} %param.20) | copy-start | bytes 1540
  14.4 0.9 %copy-start.2 = (bf16[64,1024]{1,0:T(8,128)(2,1)S(1)}, bf16[64,1024]{1,0:T(8,128)(2,1)}, u32[]{:S(2)}) copy-start(bf16[64,1024]{1,0:T(8,128)(2,1)} %param.21) | copy-start | bytes 393220
  21.1 14.0 %all-to-all-start.1 = ((bf16[32,16,128]{2,1,0:T(8,128)(2,1)}), bf16[32,16,128]{2,1,0:T(8,128)(2,1)S(1)}, u32[]{:S(2)}, u32[]{:S(2)}) async-start(bf16[32,16,128]{2,1,0:T(8,128)(2,1)} %up_root.1), calls=%async_computation.1 | async-start | bytes 262144 | tf_op jit(solution)/shard_map/all_to_all | solution.py:287
  35.1 0.6 %copy-start.1 = (bf16[32,16,128]{2,1,0:T(8,128)(2,1)}, bf16[32,16,128]{2,1,0:T(8,128)(2,1)S(1)}, u32[]{:S(2)}) copy-start(bf16[32,16,128]{2,1,0:T(8,128)(2,1)S(1)} %all-to-all-done.1.got_ref) | copy-start | bytes 393220

commit v2 on v1

v2 whole, which is shorter than its diff:
```python
import functools

import jax
import jax.numpy as jnp
from jax import lax
from jax.experimental import pallas as pl
from jax.experimental.pallas import tpu as pltpu
from jax.sharding import PartitionSpec as P

LEAF = 256
SPLIT = 256

bf16 = jnp.bfloat16
f32 = jnp.float32


def dot(a, b, over):
    return lax.dot_general(a, b, (over, ((), ())), preferred_element_type=f32)


NN = ((1,), (0,))
NT = ((1,), (1,))
TN = ((0,), (0,))


def one_hot_low(morton, width):
    rows = lax.broadcasted_iota(jnp.int32, (SPLIT, width), 0)
    return jnp.where(rows == (morton & (SPLIT - 1)), 1.0, 0.0).astype(bf16)


def window(start, points, width):
    base = jnp.minimum(start // 128 * 128, points - width)
    return pl.multiple_of(base, 128)


def spread(scr, ref, row, pitch, rank):
    flat = ref[...].astype(f32)
    n = flat.shape[0]
    for i in range(rank):
        scr[i * pitch + row : i * pitch + row + n, :rank] = flat[:, rank * i : rank * (i + 1)]


def block_of(scr, n, pitch, rank):
    return scr[pl.ds(n, rank, stride=pitch), :][:, :rank].astype(bf16)


def beside(tiles):
    return jnp.concatenate(tiles, axis=1)


def up_kernel(
    self_id,
    sizes,
    partner,
    vec_ref,
    morton_ref,
    basis_ref,
    leaf_ref,
    mid_ref,
    root_ref,
    dev_ref,
    *rest,
    few,
):
    group_refs, (coeff_ref, msg_ref, sorted_ref, leaf_scr, scr, dev_scr, group_scr) = (
        rest[:-7],
        rest[-7:],
    )
    vecs, points = vec_ref.shape
    rank = basis_ref.shape[0]
    leaves = sizes.shape[1]
    middle = mid_ref.shape[0]
    slots = dev_ref.shape[0]
    subtrees = msg_ref.shape[0]
    groups = subtrees // 8
    highs = points // SPLIT
    width = min(points, LEAF + 128)
    stacked = jnp.concatenate(
        [vec_ref[:, h * SPLIT : (h + 1) * SPLIT].astype(bf16) for h in range(highs)], axis=0
    )
    step = 256
    for k in range(points // step):
        morton = morton_ref[:, k * step : (k + 1) * step]
        mixed = dot(stacked, one_hot_low(morton, step), NN)
        high = morton // SPLIT
        picked = jnp.zeros((vecs, step), f32)
        for h in range(highs):
            picked = picked + jnp.where(high == h, mixed[h * vecs : (h + 1) * vecs], 0.0)
        sorted_ref[:, k * step : (k + 1) * step] = picked
    spread(leaf_scr, leaf_ref, 0, leaves, rank)
    spread(scr, mid_ref, 0, 8, rank)
    spread(scr, root_ref, middle, 8, rank)
    spread(dev_scr, dev_ref, 0, slots, rank)
    start = jnp.int32(0)
    mids = [jnp.zeros((vecs, rank), f32) for _ in range(middle)]
    for l in range(leaves):
        size = sizes[0, l]
        base = window(start, points, width)
        place = base + lax.broadcasted_iota(jnp.int32, (1, width), 1)
        inside = (place >= start) & (place < start + size)
        vec = jnp.where(inside, sorted_ref[:, pl.ds(base, width)], 0.0).astype(bf16)
        coeff = dot(vec, basis_ref[:, pl.ds(base, width)], NT).astype(bf16)
        coeff_ref[l] = coeff
        mids[l // 8] = mids[l // 8] + dot(coeff, block_of(leaf_scr, l, leaves, rank), NN)
        start = start + size
    root = jnp.zeros((vecs, rank), f32)
    for m in range(middle):
        root = root + dot(mids[m].astype(bf16), block_of(scr, m, 8, rank), NN)
    root = root.astype(bf16)
    term = dot(root, block_of(scr, middle, 8, rank), NN)
    blank = jnp.zeros((vecs, rank), f32)
    own = self_id[0] // 8
    if few:
        spread(group_scr, group_refs[0], 0, 8, rank)
        spread(group_scr, group_refs[1], groups, 8, rank)
        half = rank // 2
        first = self_id[0] % 2 * (half * 8)

        def half_of(h):
            mine = group_scr[pl.ds(first + h, half, stride=8), :]
            other = group_scr[pl.ds(first + groups + h, half, stride=8), :]
            return (mine + other)[:, :rank]

        below = [half_of((own + 1 + q) % groups) for q in range(1, groups - 1)]
        below = beside([part for b in below for part in (b[:8], b[8:])])
    for g in range(groups):
        if few:
            part = half_of(jnp.where(own == g, (own + 1) % groups, g))
        else:
            chunk = group_refs[0][g : g + 1, :]
            part = jnp.concatenate(
                [chunk[:, h * rank : (h + 1) * rank] for h in range(4)]
                + [jnp.zeros((vecs - 4, rank), f32)],
                axis=0,
            )
        tile = beside([root.astype(f32), term, blank, part]).astype(bf16)
        if few:
            tile = jnp.concatenate([tile, below.astype(bf16)], axis=0)
        for d in range(8):
            msg_ref[g * 8 + d] = tile
    for c in range(slots):
        who = partner[0, c]
        live = who >= 0
        where = jnp.where(live, who, self_id[0])
        back = dot(root, block_of(dev_scr, c, slots, rank), NN)
        back = jnp.where(live, back, 0.0).astype(bf16)
        msg_ref[where, :vecs, 2 * rank : 3 * rank] = back


def near_kernel(
    sizes,
    pairs,
    coeff_ref,
    morton_ref,
    basis_ref,
    leaf_ref,
    mid_ref,
    root_ref,
    dev_ref,
    couple_ref,
    reach_ref,
    near_ref,
    dev_out,
    root_out,
    leaf_scr,
    scr,
    dev_scr,
    couple_scr,
    far_scr,
    sorted_ref,
):
    rank, points = basis_ref.shape
    leaves, vecs, _ = coeff_ref.shape
    middle = mid_ref.shape[0]
    slots = dev_ref.shape[0]
    npairs = couple_ref.shape[0]
    highs = points // SPLIT
    width = min(points, LEAF + 128)
    rows = rank + vecs
    spread(leaf_scr, leaf_ref, 0, leaves, rank)
    spread(scr, mid_ref, 0, 8, rank)
    spread(scr, root_ref, middle, 8, rank)
    spread(dev_scr, dev_ref, 0, slots, rank)
    spread(couple_scr, couple_ref, 0, npairs, rank)
    dev_out[...] = beside(
        [dev_scr[pl.ds(c, rank, stride=slots), :][:, :rank] for c in range(slots)]
    ).astype(bf16)
    root_out[...] = block_of(scr, middle, 8, rank)
    far_scr[...] = jnp.zeros_like(far_scr)
    for p in range(npairs):
        a = pairs[0, p]
        b = pairs[1, p]
        block = block_of(couple_scr, p, npairs, rank)
        to_a = dot(coeff_ref[b], block, NT)
        to_b = dot(coeff_ref[a], block, NN)
        far_scr[a] += to_a
        far_scr[b] += to_b
    start = jnp.int32(0)
    for l in range(leaves):
        size = sizes[0, l]
        base = window(start, points, width)
        place = base + lax.broadcasted_iota(jnp.int32, (1, width), 1)
        inside = (place >= start) & (place < start + size)
        reach = lax.dot_general(
            block_of(scr, l // 8, 8, rank),
            block_of(leaf_scr, l, leaves, rank),
            (((0,), (1,)), ((), ())),
            preferred_element_type=f32,
        )
        both = jnp.concatenate([reach, far_scr[l]], axis=0).astype(bf16)
        value = dot(both, basis_ref[:, pl.ds(base, width)], NN)
        old = sorted_ref[:, pl.ds(base, width)]
        sorted_ref[:, pl.ds(base, width)] = jnp.where(inside, value, old)
        start = start + size
    step = 256
    result = jnp.zeros((highs * rows, SPLIT), f32)
    for k in range(points // step):
        morton = morton_ref[:, k * step : (k + 1) * step]
        high = morton // SPLIT
        value = sorted_ref[:, k * step : (k + 1) * step]
        masked = jnp.concatenate([jnp.where(high == h, value, 0.0) for h in range(highs)], axis=0)
        result = result + dot(masked.astype(bf16), one_hot_low(morton, step), NT)
    for h in range(highs):
        reach_ref[:, h * SPLIT : (h + 1) * SPLIT] = result[h * rows : h * rows + rank].astype(bf16)
        near_ref[:, h * SPLIT : (h + 1) * SPLIT] = result[h * rows + rank : (h + 1) * rows]


def last_kernel(self_id, partner, got_ref, dev_ref, root_ref, reach_ref, near_ref, out_ref, got, group_scr, *, few):
    rank = root_ref.shape[0]
    subtrees, tall, tile_lanes = got_ref.shape
    vecs = near_ref.shape[0]
    slots = dev_ref.shape[1] // rank
    groups = subtrees // 8
    own = self_id[0] // 8
    chosen = []
    for c in range(slots):
        who = partner[0, c]
        other = got_ref[jnp.maximum(who, 0)][:vecs, :rank].astype(f32)
        chosen.append(jnp.where(who >= 0, other, 0.0))
    total = dot(beside(chosen).astype(bf16), dev_ref[...], NT)
    if not few:
        got[...] = got_ref[...].astype(f32).reshape(subtrees * tall, tile_lanes)
    far = jnp.zeros((vecs, rank), f32)
    for g in range(groups):
        level = got_ref[g * 8, :vecs].astype(f32)
        for d in range(1, 8):
            level = level + got_ref[g * 8 + d, :vecs].astype(f32)
        total = total + level[:, 2 * rank : 3 * rank]
        group = level[:, rank : 2 * rank]
        if few:
            group_scr[g] = group
        else:
            pitch = groups // 4
            block = got[pl.ds(g // 4 * vecs + g % 4, rank, stride=pitch * vecs), :]
            far = far + dot(group.astype(bf16), block[:, 3 * rank : 4 * rank].astype(bf16), NT)
    if few:

        def stack_of(g, q):
            halves = []
            for core in range(2):
                acc = 0.0
                for chip in range(4):
                    message = got_ref.at[g * 8 + 2 * chip + core]
                    if q == 0:
                        part = message[:vecs, 3 * rank :].astype(f32)
                    else:
                        part = message[vecs:, (q - 1) * 2 * rank : q * 2 * rank].astype(f32)
                    acc = acc + part
                halves.append(acc if q == 0 else jnp.concatenate([acc[:, :rank], acc[:, rank:]], axis=0))
            return jnp.concatenate(halves, axis=0).astype(bf16)

        for q in range(groups - 1):
            other = (own + 1 + q) % groups
            group = group_scr[other].astype(bf16)
            far = far + dot(group, stack_of(own, q), NT) + dot(group, stack_of(other, 0), NN)
    total = (total + dot(far.astype(bf16), root_ref[...], NT)).astype(bf16)
    out_ref[...] = near_ref[...] + dot(total, reach_ref[...], NN)


smem = pl.BlockSpec(memory_space=pltpu.SMEM)
vmem = pl.BlockSpec(memory_space=pltpu.VMEM)


def body(
    vectors,
    morton_order,
    leaf_sizes,
    leaf_basis,
    leaf_transfer,
    mid_transfer,
    root_transfer,
    leaf_pairs,
    leaf_coupling,
    dev_partner,
    dev_coupling,
    grp_partner,
    grp_coupling,
):
    rank, points = leaf_basis.shape
    vecs = vectors.shape[0]
    leaves = leaf_sizes.shape[1]
    slots = dev_coupling.shape[0]
    npairs = leaf_coupling.shape[0]
    subtrees = lax.axis_size("leaf")
    groups = subtrees // 8
    few = groups == 4
    self_id = lax.axis_index("leaf").astype(jnp.int32)
    own_group = self_id // 8
    group_ids = jnp.arange(groups, dtype=jnp.int32)
    hot = (grp_partner[0][:, None] == group_ids[None, :]).astype(bf16)
    by_partner = jnp.einsum("sh,sx->hx", hot, grp_coupling, preferred_element_type=f32)
    if few:
        by_partner = by_partner.astype(bf16)
        swap = [(d, d ^ 1) for d in range(subtrees)]
        group_args = (by_partner, lax.ppermute(by_partner, "leaf", swap))
        tall = vecs + 8
    else:
        by_partner = by_partner.reshape(groups, rank, rank)
        self_hot = (group_ids == own_group).astype(f32)
        parts = (
            self_hot[:, None, None, None] * by_partner.transpose(1, 0, 2)[None]
            + self_hot[None, None, :, None] * by_partner.transpose(0, 2, 1)[:, :, None, :]
        )
        parts = parts.astype(bf16).reshape(groups, subtrees, 4 * rank).transpose(1, 0, 2)
        chunks = lax.all_to_all(parts, "leaf", 0, 0, tiled=True)
        group_args = (chunks.astype(f32).sum(0),)
        tall = vecs

    coeff, message = pl.pallas_call(
        functools.partial(up_kernel, few=few),
        out_shape=(
            jax.ShapeDtypeStruct((leaves, vecs, rank), bf16),
            jax.ShapeDtypeStruct((subtrees, tall, 4 * rank), bf16),
        ),
        in_specs=[smem] * 3 + [vmem] * (7 + len(group_args)),
        out_specs=(vmem, vmem),
        scratch_shapes=[
            pltpu.VMEM((vecs, points), f32),
            pltpu.VMEM((rank * leaves, rank), f32),
            pltpu.VMEM((rank * 8, rank), f32),
            pltpu.VMEM((rank * slots, rank), f32),
            pltpu.VMEM((rank * 8, rank), f32),
        ],
        name="up",
    )(
        self_id[None],
        leaf_sizes,
        dev_partner,
        vectors,
        morton_order,
        leaf_basis,
        leaf_transfer,
        mid_transfer,
        root_transfer,
        dev_coupling,
        *group_args,
    )
    got = lax.all_to_all(message, "leaf", 0, 0, tiled=True)

    reach, near, dev_wide, root_map = pl.pallas_call(
        near_kernel,
        out_shape=(
            jax.ShapeDtypeStruct((rank, points), bf16),
            jax.ShapeDtypeStruct((vecs, points), f32),
            jax.ShapeDtypeStruct((rank, slots * rank), bf16),
            jax.ShapeDtypeStruct((rank, rank), bf16),
        ),
        in_specs=[smem] * 2 + [vmem] * 8,
        out_specs=(vmem,) * 4,
        scratch_shapes=[
            pltpu.VMEM((rank * leaves, rank), f32),
            pltpu.VMEM((rank * 8, rank), f32),
            pltpu.VMEM((rank * slots, rank), f32),
            pltpu.VMEM((rank * npairs, rank), f32),
            pltpu.VMEM((leaves, vecs, rank), f32),
            pltpu.VMEM((rank + vecs, points), f32),
        ],
        cost_estimate=pl.CostEstimate(flops=4 << 30, bytes_accessed=4 << 20, transcendentals=0),
        name="near",
    )(
        leaf_sizes,
        leaf_pairs,
        coeff,
        morton_order,
        leaf_basis,
        leaf_transfer,
        mid_transfer,
        root_transfer,
        dev_coupling,
        leaf_coupling,
    )

    return pl.pallas_call(
        functools.partial(last_kernel, few=few),
        out_shape=jax.ShapeDtypeStruct((vecs, points), f32),
        in_specs=[smem] * 2 + [vmem] * 5,
        out_specs=vmem,
        scratch_shapes=[
            pltpu.VMEM((8 if few else subtrees * tall, 4 * rank), f32),
            pltpu.VMEM((groups, vecs, rank), f32),
        ],
        name="last",
    )(self_id[None], dev_partner, got, dev_wide, root_map, reach, near)


def solution(mesh):
    in_specs = (
        P(None, "leaf"),
        P("leaf", None),
        P("leaf", None),
        P(None, "leaf"),
        P("leaf", None),
        P("leaf", None),
        P("leaf", None),
        P(None, "leaf"),
        P("leaf", None),
        P("leaf", None),
        P("leaf", None),
        P("leaf", None),
        P("leaf", None),
    )
    out_specs = P(None, "leaf")
    return jax.shard_map(body, mesh=mesh, in_specs=in_specs, out_specs=out_specs, check_vma=False)
```

time: 40.9 us -> 27.7 us (0.68)
  Pallas kernels: 10.6 us -> 16.7 us
  starting transfers between devices: 12.9 us -> 7.14 us
  local copies, waits for them, and re-layouts: 7.31 us -> 1.96 us
  waiting for transfers between devices: 6.2 us -> 1.22 us
  matrix products: 1.78 us -> 0.26 us
  other arithmetic: 1.32 us -> 0 us
    all_to_all x1 -> x0, starting transfers between devices: 7.08 us -> none  [body(): chunks = lax.all_to_all(parts, 'leaf', 0, 0, tiled=True)]
    all_to_all x1, waiting for transfers between devices: 6.19 us -> 0.06 us  [body(): got = lax.all_to_all(message, 'leaf', 0, 0, tiled=True)]
    pallas_call x3, Pallas kernels: 10.6 us -> 16.7 us  [the longest x1 9.14 us: body(): pl.pallas_call(near_kernel, out_shape=(jax.ShapeDtypeStruct((rank, points...]
    reshape x6 -> x0, local copies, waits for them, and re-layouts: 2.59 us -> none  [the longest x1 1.1 us: body(): coeff.reshape(rank, leaves, vecs).transpose(1, 0, 2)]
    dot_general x6 -> x0, matrix products: 1.53 us -> none  [the longest x1 0.38 us: body(): jnp.einsum('pij,pjv->piv', leaf_blocks, from_second.reshape(-1, rank, vec...]
    all_to_all x1, starting transfers between devices: 5.83 us -> 7.09 us  [body(): got = lax.all_to_all(message, 'leaf', 0, 0, tiled=True)]
    ppermute x0 -> x1, waiting for transfers between devices: none -> 1.15 us  [body(): group_args = (by_partner, lax.ppermute(by_partner, 'leaf', swap))]
    transpose x2 -> x0, local copies, waits for them, and re-layouts: 1.11 us -> none  [the longest x1 1.02 us: body(): near.reshape(leaves, rank, vecs).transpose(1, 0, 2)]
  transfers between devices with their start and end apart: 2 -> 2, of which waited for: 1 -> 2; matrix products, arithmetic and copies ran while one was open for 15% -> 0% of each run, Pallas kernels for 9% -> 33%
where the time goes in v2:
time: 27.7 us; the launch traced here: 27.3 us
  Pallas kernels  16.7 us (60%)
  starting transfers between devices  7.14 us (26%)
  local copies, waits for them, and re-layouts  1.96 us (7%)
  waiting for transfers between devices  1.22 us (4%)
    pallas_call x1, Pallas kernels, body(): pl.pallas_call(near_kernel, out_shape=(jax.ShapeDtypeStruct((rank, points...  9.14 us
    all_to_all x1, starting transfers between devices, body(): got = lax.all_to_all(message, 'leaf', 0, 0, tiled=True)  7.09 us
    pallas_call x1, Pallas kernels, body(): pl.pallas_call(functools.partial(up_kernel, few=few), out_shape=(jax.Shap...  5.09 us
    pallas_call x1, Pallas kernels, body(): pl.pallas_call(functools.partial(last_kernel, few=few), out_shape=jax.Sha...  2.44 us
    unnamed x10, local copies, waits for them, and re-layouts  1.96 us
    ppermute x1, waiting for transfers between devices, body(): group_args = (by_partner, lax.ppermute(by_partner, 'leaf', swap))  1.15 us
  transfers between devices with their start and end apart: 2, of which 2 were waited for; matrix products, arithmetic and copies ran while one was open for 0% of the time, Pallas kernels for 33%

profile of v2, /device:TPU:1, one launch (start us, length us, event | category | flops | bytes accessed | tf_op | source)
XLA Modules:
  0.0 27.3 jit_solution(16414005243910914020)
XLA Ops:
  0.0 0.0 copy-start
  0.0 0.0 copy-start.4
  0.0 0.7 %copy-done = bf16[4,1024]{1,0:T(4,128)(2,1)S(1)} copy-done((bf16[4,1024]{1,0:T(4,128)(2,1)S(1)}, bf16[4,1024]{1,0:T(4,128)(2,1)}, u32[]{:S(2)}) %copy-start) | copy-done | bytes 8216
  0.7 0.0 copy-done.4
  0.7 0.3 convolution_convert_fusion.rest_0_
  1.0 0.0 copy-start.2
  1.0 0.1 collective-permute-start
  1.0 1.2 %collective-permute-done.rest_1_ = bf16[4,1024]{1,0:T(4,128)(2,1)S(1)} collective-permute-done((bf16[4,1024]{1,0:T(4,128)(2,1)S(1)}, bf16[4,1024]{1,0:T(4,128)(2,1)S(1)}, u32[]{:S(2)}, u32[]{:S(2)}) %collective-permute-start) | collective-permute-done | bytes 8224 | tf_op jit(solution)/shard_map/ppermute | solution.py:315
  2.2 0.0 copy-start.3
  2.2 0.0 copy-done.2
  2.2 0.6 %copy-done.3 = bf16[4,1024]{1,0:T(4,128)(2,1)} copy-done((bf16[4,1024]{1,0:T(4,128)(2,1)}, bf16[4,1024]{1,0:T(4,128)(2,1)S(1)}, u32[]{:S(2)}) %copy-start.3) | copy-done | bytes 8216
  2.8 5.1 %up.1 = (bf16[32,16,32]{2,1,0:T(8,128)(2,1)}, bf16[32,24,128]{2,1,0:T(8,128)(2,1)}) custom-call(s32[1]{0:T(128)} %bitcast.self_id, s32[1,32]{1,0:T(1,128)} %sizes.3, s32[1,16]{1,0:T(1,128)} %partner.3, f32[16,4096]{1,0:T(8,128)} %vec_ref.1, s32[1,4096]{1,0:T(1,128)} %morton_ref.3, bf16[32,4096]{1,0:T(8,128)(2,1)} %basis_ref.3, bf16[32,1024]{1,0:T(8,128)(2,1)} %leaf_ref.3, ...), custom_call_target="tpu_custom_call" | custom-call | tf_op jit(solution)/shard_map/up/pallas_call | solution.py:329
  7.9 7.1 %all-to-all-start = ((bf16[32,24,128]{2,1,0:T(8,128)(2,1)}), bf16[32,24,128]{2,1,0:T(8,128)(2,1)S(1)}, u32[]{:S(2)}, u32[]{:S(2)}) async-start(bf16[32,24,128]{2,1,0:T(8,128)(2,1)} %get-tuple-element.11), calls=%async_computation | async-start | bytes 393216 | tf_op jit(solution)/shard_map/all_to_all | solution.py:358
  14.9 9.1 %near.1 = (bf16[32,4096]{1,0:T(8,128)(2,1)}, f32[16,4096]{1,0:T(8,128)}, bf16[32,512]{1,0:T(8,128)(2,1)}, bf16[32,32]{1,0:T(8,128)(2,1)}) custom-call(s32[1,32]{1,0:T(1,128)} %sizes.3, s32[2,64]{1,0:T(2,128)} %pairs.1, bf16[32,16,32]{2,1,0:T(8,128)(2,1)} %get-tuple-element.12.coeff_ref, s32[1,4096]{1,0:T(1,128)} %morton_ref.3, bf16[32,4096]{1,0:T(8,128)(2,1)} %basis_ref.3, ...), custom_call_target="tpu_custom_call" | custom-call | flops 4294967296 | bytes 4194304 | tf_op jit(solution)/shard_map/near/pallas_call | solution.py:360
  24.1 0.1 all-to-all-done.got_ref
  24.1 0.0 copy-start.1
  24.2 0.7 %copy-done.1 = bf16[32,24,128]{2,1,0:T(8,128)(2,1)} copy-done((bf16[32,24,128]{2,1,0:T(8,128)(2,1)}, bf16[32,24,128]{2,1,0:T(8,128)(2,1)S(1)}, u32[]{:S(2)}) %copy-start.1) | copy-done | bytes 196632
  24.8 2.4 %last.1 = f32[16,4096]{1,0:T(8,128)} custom-call(s32[1]{0:T(128)} %bitcast.self_id, s32[1,16]{1,0:T(1,128)} %partner.3, bf16[32,24,128]{2,1,0:T(8,128)(2,1)} %copy-done.1, bf16[32,512]{1,0:T(8,128)(2,1)} %get-tuple-element.13.dev_ref, bf16[32,32]{1,0:T(8,128)(2,1)} %get-tuple-element.14.root_ref, bf16[32,4096]{1,0:T(8,128)(2,1)} %get-tuple-element.15.reach_ref, ...), custom_call_target="tpu_custom_call" | custom-call | tf_op jit(solution)/shard_map/last/pallas_call | solution.py:393
Async XLA Ops:
  0.0 0.7 %copy-start = (bf16[4,1024]{1,0:T(4,128)(2,1)S(1)}, bf16[4,1024]{1,0:T(4,128)(2,1)}, u32[]{:S(2)}) copy-start(bf16[4,1024]{1,0:T(4,128)(2,1)} %param.25) | copy-start | bytes 24580
  0.0 0.7 %copy-start.4 = (s32[1,4]{1,0:T(1,128)S(1)}, s32[1,4]{1,0:T(1,128)}, u32[]{:S(2)}) copy-start(s32[1,4]{1,0:T(1,128)} %param.24) | copy-start | bytes 52
  1.0 1.2 %copy-start.2 = (bf16[4,1024]{1,0:T(4,128)(2,1)}, bf16[4,1024]{1,0:T(4,128)(2,1)S(1)}, u32[]{:S(2)}) copy-start(bf16[4,1024]{1,0:T(4,128)(2,1)S(1)} %convolution_convert_fusion.rest_0_) | copy-start | bytes 24580
  1.0 1.2 %collective-permute-start = (bf16[4,1024]{1,0:T(4,128)(2,1)S(1)}, bf16[4,1024]{1,0:T(4,128)(2,1)S(1)}, u32[]{:S(2)}, u32[]{:S(2)}) collective-permute-start(bf16[4,1024]{1,0:T(4,128)(2,1)S(1)} %convolution_convert_fusion.rest_0_), channel_id=1, source_target_pairs={{0,1},{1,0},{2,3},{3,2},{4,5},{5,4},{6,7},{7,6},{8,9},{9,8},{10,11... | collective-permute-start | bytes 24584 | tf_op jit(solution)/shard_map/ppermute | solution.py:315
  2.2 0.6 %copy-start.3 = (bf16[4,1024]{1,0:T(4,128)(2,1)}, bf16[4,1024]{1,0:T(4,128)(2,1)S(1)}, u32[]{:S(2)}) copy-start(bf16[4,1024]{1,0:T(4,128)(2,1)S(1)} %collective-permute-done.rest_1_) | copy-start | bytes 24580
  7.9 16.3 %all-to-all-start = ((bf16[32,24,128]{2,1,0:T(8,128)(2,1)}), bf16[32,24,128]{2,1,0:T(8,128)(2,1)S(1)}, u32[]{:S(2)}, u32[]{:S(2)}) async-start(bf16[32,24,128]{2,1,0:T(8,128)(2,1)} %get-tuple-element.11), calls=%async_computation | async-start | bytes 393216 | tf_op jit(solution)/shard_map/all_to_all | solution.py:358
  24.1 0.7 %copy-start.1 = (bf16[32,24,128]{2,1,0:T(8,128)(2,1)}, bf16[32,24,128]{2,1,0:T(8,128)(2,1)S(1)}, u32[]{:S(2)}) copy-start(bf16[32,24,128]{2,1,0:T(8,128)(2,1)S(1)} %all-to-all-done.got_ref) | copy-start | bytes 589828

commit v3 on v2

v3 whole, which is shorter than its diff:
```python
import functools

import jax
import jax.numpy as jnp
from jax import lax
from jax.experimental import pallas as pl
from jax.experimental.pallas import tpu as pltpu
from jax.sharding import PartitionSpec as P

LEAF = 256
SPLIT = 256

bf16 = jnp.bfloat16
f32 = jnp.float32


def dot(a, b, over):
    return lax.dot_general(a, b, (over, ((), ())), preferred_element_type=f32)


NN = ((1,), (0,))
NT = ((1,), (1,))
TN = ((0,), (0,))


def one_hot_low(morton, width):
    rows = lax.broadcasted_iota(jnp.int32, (SPLIT, width), 0).astype(bf16)
    low = (morton & (SPLIT - 1)).astype(f32).astype(bf16)
    return jnp.where(rows == low, jnp.ones((), bf16), jnp.zeros((), bf16))


def window(start, points, width):
    base = jnp.minimum(start - (start & 127), points - width)
    return pl.multiple_of(base, 128)


def inside_of(start, size, base, shape):
    place = lax.broadcasted_iota(jnp.int32, shape, 1) + (base - start)
    return place.astype(jnp.uint32) < size.astype(jnp.uint32)


def pitch_of(n):
    return n + 8 if n % 16 == 0 else n


def spread(scr, ref, row, pitch, rank):
    flat = ref[...].astype(f32)
    n = flat.shape[0]
    for i in range(rank):
        scr[i * pitch + row : i * pitch + row + n, :rank] = flat[:, rank * i : rank * (i + 1)]


def block_of(scr, n, pitch, rank):
    return scr[pl.ds(n, rank, stride=pitch), :][:, :rank].astype(bf16)


def beside(tiles):
    return jnp.concatenate(tiles, axis=1)


def up_kernel(
    sizes_hbm,
    partner_hbm,
    vec_hbm,
    morton_hbm,
    basis_hbm,
    leaf_hbm,
    mid_hbm,
    root_hbm,
    dev_hbm,
    who_hbm,
    group_hbm,
    coeff_ref,
    tops_ref,
    back_ref,
    who_ref,
    group_ref,
    sizes,
    partner,
    vec_ref,
    morton_ref,
    basis_ref,
    leaf_ref,
    mid_ref,
    root_ref,
    dev_ref,
    sems,
    sorted_ref,
    leaf_scr,
    scr,
    dev_scr,
):
    vecs, points = vec_ref.shape
    rank = basis_ref.shape[0]
    leaves = sizes.shape[1]
    middle = mid_ref.shape[0]
    slots = dev_ref.shape[0]
    highs = points // SPLIT
    width = min(points, LEAF + 128)
    copies = [
        pltpu.make_async_copy(src, dst, sems.at[n])
        for n, (src, dst) in enumerate(
            (
                (morton_hbm, morton_ref),
                (vec_hbm, vec_ref),
                (basis_hbm, basis_ref),
                (leaf_hbm, leaf_ref),
                (mid_hbm, mid_ref),
                (root_hbm, root_ref),
                (dev_hbm, dev_ref),
                (sizes_hbm, sizes),
                (partner_hbm, partner),
                (who_hbm, who_ref),
                (group_hbm, group_ref),
            )
        )
    ]
    for copy in copies:
        copy.start()
    copies[0].wait()
    copies[1].wait()
    stacked = jnp.concatenate(
        [vec_ref[:, h * SPLIT : (h + 1) * SPLIT].astype(bf16) for h in range(highs)], axis=0
    )
    step = 256
    for k in range(points // step):
        morton = morton_ref[:, k * step : (k + 1) * step]
        mixed = dot(stacked, one_hot_low(morton, step), NN)
        high = morton // SPLIT
        picked = mixed[:vecs]
        for h in range(1, highs):
            picked = jnp.where(high == h, mixed[h * vecs : (h + 1) * vecs], picked)
        sorted_ref[:, k * step : (k + 1) * step] = picked
    for copy in copies[2:]:
        copy.wait()
    spread(leaf_scr, leaf_ref, 0, pitch_of(leaves), rank)
    spread(scr, mid_ref, 0, 8, rank)
    spread(scr, root_ref, middle, 8, rank)
    spread(dev_scr, dev_ref, 0, pitch_of(slots), rank)
    back_ref[...] = jnp.zeros_like(back_ref)
    start = jnp.int32(0)
    coeffs = []
    for l in range(leaves):
        size = sizes[0, l]
        base = window(start, points, width)
        inside = inside_of(start, size, base, (vecs, width))
        vec = jnp.where(inside, sorted_ref[:, pl.ds(base, width)], 0.0).astype(bf16)
        coeff = dot(vec, basis_ref[:, pl.ds(base, width)], NT)
        coeff_ref[l] = coeff.astype(bf16)
        coeffs.append(coeff)
        start = start + size
    mids = []
    for m in range(middle):
        kids = range(8 * m, 8 * m + 8)
        maps = [block_of(leaf_scr, l, pitch_of(leaves), rank) for l in kids]
        maps = jnp.concatenate(maps, axis=0)
        mids.append(dot(beside([coeffs[l] for l in kids]).astype(bf16), maps, NN))
    maps = jnp.concatenate([block_of(scr, m, 8, rank) for m in range(middle)], axis=0)
    root = dot(beside(mids).astype(bf16), maps, NN).astype(bf16)
    term = dot(root, block_of(scr, middle, 8, rank), NN)
    tops_ref[...] = beside([root.astype(f32), term])
    self_id = lax.axis_index("leaf")
    for c in range(slots):
        who = partner[0, c]
        back = dot(root, block_of(dev_scr, c, pitch_of(slots), rank), NN)
        back_ref[jnp.where(who >= 0, who, self_id)] = jnp.where(who >= 0, back, 0.0)


def pack_kernel(tops_ref, back_ref, *rest, few):
    group_refs, (msg_hbm, msg_ref, group_scr, half_scr, sems) = rest[:-5], rest[-5:]
    vecs = tops_ref.shape[0]
    rank = tops_ref.shape[1] // 2
    subtrees = msg_ref.shape[0]
    groups = subtrees // 8
    self_id = lax.axis_index("leaf")
    own = self_id // 8
    copies = []
    if few:
        held = group_refs[2].shape[0]
        pitch = 2 * held
        spread(group_scr, group_refs[2], 0, pitch, rank)
        spread(group_scr, group_refs[3], held, pitch, rank)
        half = rank // 2
        first = self_id % 2 * (half * pitch)
        sums = [jnp.zeros((half, rank), f32) for _ in range(groups)]
        for s in range(pitch):
            target = group_refs[s // held][:, s % held : s % held + 1]
            block = group_scr[pl.ds(first + s, half, stride=pitch), :][:, :rank]
            for h in range(groups):
                sums[h] = sums[h] + jnp.where(target == h, block, 0.0)
        for h in range(groups):
            half_scr[h] = sums[h]
        below = [half_scr[(own + 1 + q) % groups] for q in range(1, groups - 1)]
        below = beside([part for b in below for part in (b[:8], b[8:])]).astype(bf16)
    blank = jnp.zeros((vecs, rank), f32)
    for g in range(groups):
        if few:
            part = half_scr[jnp.where(own == g, (own + 1) % groups, g)]
        else:
            chunk = group_refs[0][g : g + 1, :]
            part = jnp.concatenate(
                [chunk[:, h * rank : (h + 1) * rank] for h in range(4)]
                + [jnp.zeros((vecs - 4, rank), f32)],
                axis=0,
            )
        tile = beside([tops_ref[...], blank, part]).astype(bf16)
        if few:
            tile = jnp.concatenate([tile, below], axis=0)
        for d in range(8 * g, 8 * g + 8):
            msg_ref[d] = tile
            msg_ref[d, :vecs, 2 * rank : 3 * rank] = back_ref[d].astype(bf16)
        some = pl.ds(8 * g, 8)
        copies.append(pltpu.make_async_copy(msg_ref.at[some], msg_hbm.at[some], sems.at[g]))
        copies[-1].start()
    for copy in copies:
        copy.wait()


def near_kernel(
    sizes,
    pairs,
    partner,
    coeff_ref,
    morton_ref,
    basis_ref,
    leaf_ref,
    mid_ref,
    root_ref,
    dev_ref,
    couple_ref,
    reach_ref,
    near_ref,
    dev_out,
    root_out,
    leaf_scr,
    scr,
    dev_scr,
    couple_scr,
    far_scr,
    sorted_ref,
    wide_scr,
):
    rank, points = basis_ref.shape
    leaves, vecs, _ = coeff_ref.shape
    middle = mid_ref.shape[0]
    slots = dev_ref.shape[0]
    npairs = couple_ref.shape[0]
    highs = points // SPLIT
    width = min(points, LEAF + 128)
    rows = rank + vecs
    spread(leaf_scr, leaf_ref, 0, pitch_of(leaves), rank)
    spread(scr, mid_ref, 0, 8, rank)
    spread(scr, root_ref, middle, 8, rank)
    spread(dev_scr, dev_ref, 0, pitch_of(slots), rank)
    spread(couple_scr, couple_ref, 0, pitch_of(npairs), rank)
    same = lax.broadcasted_iota(jnp.int32, (rank, 4 * rank), 1)
    same = same == lax.broadcasted_iota(jnp.int32, (rank, 4 * rank), 0) + 2 * rank
    same = jnp.where(same, 1.0, 0.0)
    subtrees = wide_scr.shape[0] - 1
    for b in range(subtrees):
        wide_scr[b] = same
    for c in range(slots):
        who = partner[0, c]
        block = dev_scr[pl.ds(c, rank, stride=pitch_of(slots)), :][:, :rank]
        wide_scr[jnp.where(who >= 0, who, subtrees), :, :rank] = block
    for b in range(subtrees):
        dev_out[:, 4 * rank * b : 4 * rank * (b + 1)] = wide_scr[b].astype(bf16)
    root_out[...] = block_of(scr, middle, 8, rank)
    far_scr[...] = jnp.zeros_like(far_scr)
    for p in range(npairs):
        a = pairs[0, p]
        b = pairs[1, p]
        block = block_of(couple_scr, p, pitch_of(npairs), rank)
        to_a = dot(coeff_ref[b], block, NT)
        to_b = dot(coeff_ref[a], block, NN)
        far_scr[a] += to_a
        far_scr[b] += to_b
    start = jnp.int32(0)
    for l in range(leaves):
        size = sizes[0, l]
        base = window(start, points, width)
        inside = inside_of(start, size, base, (rows, width))
        reach = lax.dot_general(
            block_of(scr, l // 8, 8, rank),
            block_of(leaf_scr, l, pitch_of(leaves), rank),
            (((0,), (1,)), ((), ())),
            preferred_element_type=f32,
        )
        both = jnp.concatenate([reach, far_scr[l]], axis=0).astype(bf16)
        value = dot(both, basis_ref[:, pl.ds(base, width)], NN)
        old = sorted_ref[:, pl.ds(base, width)]
        sorted_ref[:, pl.ds(base, width)] = jnp.where(inside, value, old)
        start = start + size
    step = 256
    result = jnp.zeros((highs * rows, SPLIT), f32)
    for k in range(points // step):
        morton = morton_ref[:, k * step : (k + 1) * step]
        high = morton // SPLIT
        value = sorted_ref[:, k * step : (k + 1) * step]
        masked = jnp.concatenate([jnp.where(high == h, value, 0.0) for h in range(highs)], axis=0)
        result = result + dot(masked.astype(bf16), one_hot_low(morton, step), NT)
    for h in range(highs):
        reach_ref[:, h * SPLIT : (h + 1) * SPLIT] = result[h * rows : h * rows + rank].astype(bf16)
        near_ref[:, h * SPLIT : (h + 1) * SPLIT] = result[h * rows + rank : (h + 1) * rows]


def last_kernel(
    got_ref,
    dev_ref,
    root_ref,
    reach_ref,
    near_ref,
    out_hbm,
    got,
    group_scr,
    out_ref,
    sems,
    *,
    few,
):
    rank = root_ref.shape[0]
    subtrees, tall, tile_lanes = got_ref.shape
    vecs = near_ref.shape[0]
    groups = subtrees // 8
    own = lax.axis_index("leaf") // 8
    total = dot(beside([got_ref[b][:vecs] for b in range(subtrees)]), dev_ref[...], NT)
    if not few:
        got[...] = got_ref[...].astype(f32).reshape(subtrees * tall, tile_lanes)
    far = jnp.zeros((vecs, rank), f32)
    for g in range(groups):
        level = got_ref[g * 8, :vecs].astype(f32)
        for d in range(1, 8):
            level = level + got_ref[g * 8 + d, :vecs].astype(f32)
        group = level[:, rank : 2 * rank]
        if few:
            group_scr[g] = group
        else:
            pitch = groups // 4
            block = got[pl.ds(g // 4 * vecs + g % 4, rank, stride=pitch * vecs), :]
            far = far + dot(group.astype(bf16), block[:, 3 * rank : 4 * rank].astype(bf16), NT)
    if few:

        def stack_of(g, q):
            halves = []
            for core in range(2):
                acc = 0.0
                for chip in range(4):
                    message = got_ref.at[g * 8 + 2 * chip + core]
                    if q == 0:
                        part = message[:vecs, 3 * rank :].astype(f32)
                    else:
                        part = message[vecs:, (q - 1) * 2 * rank : q * 2 * rank].astype(f32)
                    acc = acc + part
                halves.append(acc if q == 0 else jnp.concatenate([acc[:, :rank], acc[:, rank:]], axis=0))
            return jnp.concatenate(halves, axis=0).astype(bf16)

        for q in range(groups - 1):
            other = (own + 1 + q) % groups
            group = group_scr[other].astype(bf16)
            far = far + dot(group, stack_of(own, q), NT) + dot(group, stack_of(other, 0), NN)
    total = (total + dot(far.astype(bf16), root_ref[...], NT)).astype(bf16)
    points = near_ref.shape[1]
    pieces = sems.shape[0]
    copies = []
    for n in range(pieces):
        cols = pl.ds(n * (points // pieces), points // pieces)
        out_ref[:, cols] = near_ref[:, cols] + dot(total, reach_ref[:, cols], NN)
        copies.append(pltpu.make_async_copy(out_ref.at[:, cols], out_hbm.at[:, cols], sems.at[n]))
        copies[-1].start()
    for copy in copies:
        copy.wait()


smem = pl.BlockSpec(memory_space=pltpu.SMEM)
vmem = pl.BlockSpec(memory_space=pltpu.VMEM)


def on_chip(x):
    return pltpu.with_memory_space_constraint(x, pltpu.VMEM)


def body(
    vectors,
    morton_order,
    leaf_sizes,
    leaf_basis,
    leaf_transfer,
    mid_transfer,
    root_transfer,
    leaf_pairs,
    leaf_coupling,
    dev_partner,
    dev_coupling,
    grp_partner,
    grp_coupling,
):
    rank, points = leaf_basis.shape
    vecs = vectors.shape[0]
    leaves = leaf_sizes.shape[1]
    slots = dev_coupling.shape[0]
    npairs = leaf_coupling.shape[0]
    subtrees = lax.axis_size("leaf")
    groups = subtrees // 8
    few = groups == 4
    keep, made = (on_chip, pltpu.VMEM) if few else (lambda x: x, jax.ShapeDtypeStruct)
    self_id = lax.axis_index("leaf").astype(jnp.int32)
    own_group = self_id // 8
    group_ids = jnp.arange(groups, dtype=jnp.int32)
    if few:
        swap = [(d, d ^ 1) for d in range(subtrees)]
        their_who = lax.ppermute(grp_partner, "leaf", swap)
        their_blocks = lax.ppermute(grp_coupling, "leaf", swap)
        tall = vecs + 8
    else:
        hot = (grp_partner[0][:, None] == group_ids[None, :]).astype(bf16)
        by_partner = jnp.einsum("sh,sx->hx", hot, grp_coupling, preferred_element_type=f32)
        by_partner = by_partner.reshape(groups, rank, rank)
        self_hot = (group_ids == own_group).astype(f32)
        parts = (
            self_hot[:, None, None, None] * by_partner.transpose(1, 0, 2)[None]
            + self_hot[None, None, :, None] * by_partner.transpose(0, 2, 1)[:, :, None, :]
        )
        parts = parts.astype(bf16).reshape(groups, subtrees, 4 * rank).transpose(1, 0, 2)
        chunks = lax.all_to_all(parts, "leaf", 0, 0, tiled=True)
        chunk = chunks.astype(f32).sum(0)
        tall = vecs

    coeff, tops, backs, own_who, own_blocks = pl.pallas_call(
        up_kernel,
        out_shape=(
            made((leaves, vecs, rank), bf16),
            made((vecs, 2 * rank), f32),
            made((subtrees, vecs, rank), f32),
            made(grp_partner.shape, grp_partner.dtype),
            made(grp_coupling.shape, grp_coupling.dtype),
        ),
        in_specs=[pl.BlockSpec(memory_space=pl.ANY)] * 11,
        out_specs=(vmem,) * 5,
        scratch_shapes=[pltpu.SMEM(x.shape, x.dtype) for x in (leaf_sizes, dev_partner)]
        + [
            pltpu.VMEM(x.shape, x.dtype)
            for x in (
                vectors,
                morton_order,
                leaf_basis,
                leaf_transfer,
                mid_transfer,
                root_transfer,
                dev_coupling,
            )
        ]
        + [
            pltpu.SemaphoreType.DMA((11,)),
            pltpu.VMEM((vecs, points), f32),
            pltpu.VMEM((rank * pitch_of(leaves), rank), f32),
            pltpu.VMEM((rank * 8, rank), f32),
            pltpu.VMEM((rank * pitch_of(slots), rank), f32),
        ],
        cost_estimate=pl.CostEstimate(flops=2 << 30, bytes_accessed=1 << 20, transcendentals=0),
        name="up",
    )(
        leaf_sizes,
        dev_partner,
        vectors,
        morton_order,
        leaf_basis,
        leaf_transfer,
        mid_transfer,
        root_transfer,
        dev_coupling,
        grp_partner,
        grp_coupling,
    )
    if few:
        group_args = [keep(x) for x in (own_who, their_who, own_blocks, their_blocks)]
    else:
        group_args = [chunk]
    message = pl.pallas_call(
        functools.partial(pack_kernel, few=few),
        out_shape=jax.ShapeDtypeStruct((subtrees, tall, 4 * rank), bf16),
        in_specs=[vmem] * (2 + len(group_args)),
        out_specs=pl.BlockSpec(memory_space=pl.ANY),
        scratch_shapes=[
            pltpu.VMEM((subtrees, tall, 4 * rank), bf16),
            pltpu.VMEM((rank * 2 * grp_coupling.shape[0], rank), f32),
            pltpu.VMEM((groups, rank // 2, rank), f32),
            pltpu.SemaphoreType.DMA((groups,)),
        ],
        name="pack",
    )(keep(tops), keep(backs), *group_args)
    got = lax.all_to_all(message, "leaf", 0, 0, tiled=True)

    reach, near, dev_wide, root_map = pl.pallas_call(
        near_kernel,
        out_shape=(
            made((rank, points), bf16),
            made((vecs, points), f32),
            made((rank, subtrees * 4 * rank), bf16),
            made((rank, rank), bf16),
        ),
        in_specs=[smem] * 3 + [vmem] * 8,
        out_specs=(vmem,) * 4,
        scratch_shapes=[
            pltpu.VMEM((rank * pitch_of(leaves), rank), f32),
            pltpu.VMEM((rank * 8, rank), f32),
            pltpu.VMEM((rank * pitch_of(slots), rank), f32),
            pltpu.VMEM((rank * pitch_of(npairs), rank), f32),
            pltpu.VMEM((leaves, vecs, rank), f32),
            pltpu.VMEM((rank + vecs, points), f32),
            pltpu.VMEM((subtrees + 1, rank, 4 * rank), f32),
        ],
        cost_estimate=pl.CostEstimate(flops=4 << 30, bytes_accessed=4 << 20, transcendentals=0),
        name="near",
    )(
        leaf_sizes,
        leaf_pairs,
        dev_partner,
        keep(coeff),
        keep(morton_order),
        keep(leaf_basis),
        keep(leaf_transfer),
        keep(mid_transfer),
        keep(root_transfer),
        keep(dev_coupling),
        keep(leaf_coupling),
    )

    return pl.pallas_call(
        functools.partial(last_kernel, few=few),
        out_shape=jax.ShapeDtypeStruct((vecs, points), f32),
        in_specs=[vmem] * 5,
        out_specs=pl.BlockSpec(memory_space=pl.ANY),
        scratch_shapes=[
            pltpu.VMEM((8 if few else subtrees * tall, 4 * rank), f32),
            pltpu.VMEM((groups, vecs, rank), f32),
            pltpu.VMEM((vecs, points), f32),
            pltpu.SemaphoreType.DMA((4,)),
        ],
        name="last",
    )(
        keep(got),
        keep(dev_wide),
        keep(root_map),
        keep(reach),
        keep(near),
    )


def solution(mesh):
    in_specs = (
        P(None, "leaf"),
        P("leaf", None),
        P("leaf", None),
        P(None, "leaf"),
        P("leaf", None),
        P("leaf", None),
        P("leaf", None),
        P(None, "leaf"),
        P("leaf", None),
        P("leaf", None),
        P("leaf", None),
        P("leaf", None),
        P("leaf", None),
    )
    out_specs = P(None, "leaf")
    return jax.shard_map(body, mesh=mesh, in_specs=in_specs, out_specs=out_specs, check_vma=False)
```

time: 27.7 us -> 22.2 us (0.80)
  Pallas kernels: 16.7 us -> 12.6 us
  local copies, waits for them, and re-layouts: 1.96 us -> 0.04 us
  starting transfers between devices: 7.14 us -> 7.6 us
  waiting for transfers between devices: 1.22 us -> 1.52 us
    pallas_call x2 -> x3, Pallas kernels: 14.2 us -> 11.4 us  [the longest x1 7.62 us: body(): pl.pallas_call(near_kernel, out_shape=(made((rank, points), bf16), made((...]
    unnamed x10 -> x14, local copies, waits for them, and re-layouts: 1.96 us -> 0.04 us
    all_to_all x1, waiting for transfers between devices: 0.06 us -> 1.51 us  [body(): got = lax.all_to_all(message, 'leaf', 0, 0, tiled=True)]
    pallas_call x1, Pallas kernels: 2.44 us -> 1.27 us  [body(): pl.pallas_call(functools.partial(last_kernel, few=few), out_shape=jax.Sha...]
    ppermute x1 -> x2, waiting for transfers between devices: 1.15 us -> 0.01 us  [the longest x1 0.01 us: body(): their_blocks = lax.ppermute(grp_coupling, 'leaf', swap)]
    ppermute x1 -> x2, starting transfers between devices: 0.06 us -> 0.51 us  [the longest x1 0.49 us: body(): their_blocks = lax.ppermute(grp_coupling, 'leaf', swap)]
  transfers between devices with their start and end apart: 2 -> 3, of which waited for: 2 -> 1; matrix products, arithmetic and copies ran while one was open for 0% -> 0% of each run, Pallas kernels for 33% -> 48%
where the time goes in v3:
time: 22.2 us; the launch traced here: 21.9 us
  Pallas kernels  12.6 us (57%)
  starting transfers between devices  7.6 us (34%)
  waiting for transfers between devices  1.52 us (7%)
    pallas_call x1, Pallas kernels, body(): pl.pallas_call(near_kernel, out_shape=(made((rank, points), bf16), made((...  7.62 us
    all_to_all x1, starting transfers between devices, body(): got = lax.all_to_all(message, 'leaf', 0, 0, tiled=True)  7.09 us
    pallas_call x1, Pallas kernels, body(): pl.pallas_call(up_kernel, out_shape=(made((leaves, vecs, rank), bf16), ma...  2.8 us
    all_to_all x1, waiting for transfers between devices, body(): got = lax.all_to_all(message, 'leaf', 0, 0, tiled=True)  1.51 us
    pallas_call x1, Pallas kernels, body(): pl.pallas_call(functools.partial(last_kernel, few=few), out_shape=jax.Sha...  1.27 us
    pallas_call x1, Pallas kernels, body(): pl.pallas_call(functools.partial(pack_kernel, few=few), out_shape=jax.Sha...  0.93 us
    ppermute x1, starting transfers between devices, body(): their_blocks = lax.ppermute(grp_coupling, 'leaf', swap)  0.49 us
  transfers between devices with their start and end apart: 3, of which 1 were waited for; matrix products, arithmetic and copies ran while one was open for 0% of the time, Pallas kernels for 48%

profile of v3, /device:TPU:1, one launch (start us, length us, event | category | flops | bytes accessed | tf_op | source)
XLA Modules:
  0.0 21.9 jit_solution(4793370304155528071)
XLA Ops:
  0.0 0.0 collective-permute-start
  0.0 0.5 %collective-permute-start.1 = (bf16[4,1024]{1,0:T(4,128)(2,1)}, bf16[4,1024]{1,0:T(4,128)(2,1)S(1)}, u32[]{:S(2)}, u32[]{:S(2)}) collective-permute-start(bf16[4,1024]{1,0:T(4,128)(2,1)} %group_hbm.1), channel_id=1, source_target_pairs={{0,1},{1,0},{2,3},{3,2},{4,5},{5,4},{6,7},{7,6},{8,9},{9,8},{10,11... | collective-permute-start | bytes 24584 | tf_op jit(solution)/shard_map/ppermute | solution.py:412
  0.5 2.8 %up.1 = (bf16[32,16,32]{2,1,0:T(8,128)(2,1)S(1)}, f32[16,64]{1,0:T(8,128)S(1)}, f32[32,16,32]{2,1,0:T(8,128)S(1)}, s32[1,4]{1,0:T(1,128)S(1)}, bf16[4,1024]{1,0:T(4,128)(2,1)S(1)}) custom-call(s32[1,32]{1,0:T(1,128)} %sizes.1, s32[1,16]{1,0:T(1,128)} %partner.1, f32[16,4096]{1,0:T(8,128)} %vec_hbm.1, s32[1,4096]{1,0:T(1,128)} %morton_ref.1, ...), custom_call_target="tpu_custom_call" | custom-call | flops 2147483648 | bytes 1048576 | tf_op jit(solution)/shard_map/up/pallas_call | solution.py:428
  3.3 0.0 collective-permute-done.rest_1_
  3.3 0.0 collective-permute-done.1.rest_3_
  3.3 0.0 copy-start.2
  3.4 0.0 copy-start.3
  3.4 0.0 copy-start.4
  3.4 0.0 copy-start.5
  3.4 0.0 copy-start.6
  3.4 0.9 %pack.1 = bf16[32,24,128]{2,1,0:T(8,128)(2,1)} custom-call(f32[16,64]{1,0:T(8,128)S(1)} %get-tuple-element.14.tops_ref, f32[32,16,32]{2,1,0:T(8,128)S(1)} %get-tuple-element.15.back_ref, s32[1,4]{1,0:T(1,128)S(1)} %get-tuple-element.16.rest_0_, s32[1,4]{1,0:T(1,128)S(1)} %collective-permute-done.rest_1_, bf16[4,1024]{1,0:T(4,128)(2,1)S(1)} %get-tuple-element.17.rest_2_, ...), custom_call_target="tpu_custom_call" | custom-call | tf_op jit(solution)/shard_map/pack/pallas_call | solution.py:478
  4.3 0.0 copy-start
  4.4 0.0 copy-start.1
  4.4 7.1 %all-to-all-start = ((bf16[32,24,128]{2,1,0:T(8,128)(2,1)}), bf16[32,24,128]{2,1,0:T(8,128)(2,1)S(1)}, u32[]{:S(2)}, u32[]{:S(2)}) async-start(bf16[32,24,128]{2,1,0:T(8,128)(2,1)} %pack.1), calls=%async_computation | async-start | bytes 393216 | tf_op jit(solution)/shard_map/all_to_all | solution.py:491
  11.5 0.0 copy-done.2
  11.5 0.0 copy-done.3
  11.5 0.0 copy-done.4
  11.5 0.0 copy-done.5
  11.5 0.0 copy-done.6
  11.5 0.0 copy-done
  11.5 0.0 copy-done.1
  11.5 7.6 %near.1 = (bf16[32,4096]{1,0:T(8,128)(2,1)S(1)}, f32[16,4096]{1,0:T(8,128)S(1)}, bf16[32,4096]{1,0:T(8,128)(2,1)S(1)}, bf16[32,32]{1,0:T(8,128)(2,1)S(1)}) custom-call(s32[1,32]{1,0:T(1,128)} %sizes.1, s32[2,64]{1,0:T(2,128)} %pairs.1, s32[1,16]{1,0:T(1,128)} %partner.1, bf16[32,16,32]{2,1,0:T(8,128)(2,1)S(1)} %get-tuple-element.18.coeff_ref, ...), custom_call_target="tpu_custom_call" | custom-call | flops 4294967296 | bytes 4194304 | tf_op jit(solution)/shard_map/near/pallas_call | solution.py:493
  19.2 1.5 %all-to-all-done.got_ref = bf16[32,24,128]{2,1,0:T(8,128)(2,1)S(1)} async-done(((bf16[32,24,128]{2,1,0:T(8,128)(2,1)}), bf16[32,24,128]{2,1,0:T(8,128)(2,1)S(1)}, u32[]{:S(2)}, u32[]{:S(2)}) %all-to-all-start) | async-done | bytes 196640 | tf_op jit(solution)/shard_map/all_to_all | solution.py:491
  20.7 1.3 %last.1 = f32[16,4096]{1,0:T(8,128)} custom-call(bf16[32,24,128]{2,1,0:T(8,128)(2,1)S(1)} %all-to-all-done.got_ref, bf16[32,4096]{1,0:T(8,128)(2,1)S(1)} %get-tuple-element.19.dev_ref, bf16[32,32]{1,0:T(8,128)(2,1)S(1)} %get-tuple-element.20.root_ref, bf16[32,4096]{1,0:T(8,128)(2,1)S(1)} %get-tuple-element.21.reach_ref, ...), custom_call_target="tpu_custom_call" | custom-call | tf_op jit(solution)/shard_map/last/pallas_call | solution.py:528
Async XLA Ops:
  0.0 3.3 %collective-permute-start = (s32[1,4]{1,0:T(1,128)}, s32[1,4]{1,0:T(1,128)S(1)}, u32[]{:S(2)}, u32[]{:S(2)}) collective-permute-start(s32[1,4]{1,0:T(1,128)} %who_hbm.1), channel_id=1, source_target_pairs={{0,1},{1,0},{2,3},{3,2},{4,5},{5,4},{6,7},{7,6},{8,9},{9,8},{10,11... | collective-permute-start | bytes 56 | tf_op jit(solution)/shard_map/ppermute | solution.py:411
  0.0 3.3 %collective-permute-start.1 = (bf16[4,1024]{1,0:T(4,128)(2,1)}, bf16[4,1024]{1,0:T(4,128)(2,1)S(1)}, u32[]{:S(2)}, u32[]{:S(2)}) collective-permute-start(bf16[4,1024]{1,0:T(4,128)(2,1)} %group_hbm.1), channel_id=1, source_target_pairs={{0,1},{1,0},{2,3},{3,2},{4,5},{5,4},{6,7},{7,6},{8,9},{9,8},{10,11... | collective-permute-start | bytes 24584 | tf_op jit(solution)/shard_map/ppermute | solution.py:412
  3.3 8.1 %copy-start.2 = (bf16[32,1024]{1,0:T(8,128)(2,1)S(1)}, bf16[32,1024]{1,0:T(8,128)(2,1)}, u32[]{:S(2)}) copy-start(bf16[32,1024]{1,0:T(8,128)(2,1)} %leaf_ref.1) | copy-start | bytes 196612
  3.4 8.1 %copy-start.3 = (bf16[16,1024]{1,0:T(8,128)(2,1)S(1)}, bf16[16,1024]{1,0:T(8,128)(2,1)}, u32[]{:S(2)}) copy-start(bf16[16,1024]{1,0:T(8,128)(2,1)} %dev_ref.1) | copy-start | bytes 98308
  3.4 8.1 %copy-start.4 = (s32[1,4096]{1,0:T(1,128)S(1)}, s32[1,4096]{1,0:T(1,128)}, u32[]{:S(2)}) copy-start(s32[1,4096]{1,0:T(1,128)} %morton_ref.1) | copy-start | bytes 49156
  3.4 8.1 %copy-start.5 = (bf16[4,1024]{1,0:T(4,128)(2,1)S(1)}, bf16[4,1024]{1,0:T(4,128)(2,1)}, u32[]{:S(2)}) copy-start(bf16[4,1024]{1,0:T(4,128)(2,1)} %mid_ref.1) | copy-start | bytes 24580
  3.4 8.1 %copy-start.6 = (bf16[1,1024]{1,0:T(2,128)(2,1)S(1)}, bf16[1,1024]{1,0:T(2,128)(2,1)}, u32[]{:S(2)}) copy-start(bf16[1,1024]{1,0:T(2,128)(2,1)} %root_ref.1) | copy-start | bytes 6148
  4.3 7.2 %copy-start = (bf16[32,4096]{1,0:T(8,128)(2,1)S(1)}, bf16[32,4096]{1,0:T(8,128)(2,1)}, u32[]{:S(2)}) copy-start(bf16[32,4096]{1,0:T(8,128)(2,1)} %basis_ref.1) | copy-start | bytes 786436
  4.4 7.2 %copy-start.1 = (bf16[64,1024]{1,0:T(8,128)(2,1)S(1)}, bf16[64,1024]{1,0:T(8,128)(2,1)}, u32[]{:S(2)}) copy-start(bf16[64,1024]{1,0:T(8,128)(2,1)} %couple_ref.1) | copy-start | bytes 393220
  4.4 16.3 %all-to-all-start = ((bf16[32,24,128]{2,1,0:T(8,128)(2,1)}), bf16[32,24,128]{2,1,0:T(8,128)(2,1)S(1)}, u32[]{:S(2)}, u32[]{:S(2)}) async-start(bf16[32,24,128]{2,1,0:T(8,128)(2,1)} %pack.1), calls=%async_computation | async-start | bytes 393216 | tf_op jit(solution)/shard_map/all_to_all | solution.py:491

commit v4 on v3

--- a/solution.py
+++ b/solution.py
@@ -97,28 +97,32 @@
     slots = dev_ref.shape[0]
     highs = points // SPLIT
     width = min(points, LEAF + 128)
+    basis_copy = pltpu.make_async_copy(basis_hbm, basis_ref, sems.at[1])
     copies = [
-        pltpu.make_async_copy(src, dst, sems.at[n])
-        for n, (src, dst) in enumerate(
-            (
-                (morton_hbm, morton_ref),
-                (vec_hbm, vec_ref),
-                (basis_hbm, basis_ref),
-                (leaf_hbm, leaf_ref),
-                (mid_hbm, mid_ref),
-                (root_hbm, root_ref),
-                (dev_hbm, dev_ref),
-                (sizes_hbm, sizes),
-                (partner_hbm, partner),
-                (who_hbm, who_ref),
-                (group_hbm, group_ref),
-            )
+        pltpu.make_async_copy(src, dst, sems.at[0])
+        for src, dst in (
+            (vec_hbm, vec_ref),
+            (morton_hbm, morton_ref),
+            (sizes_hbm, sizes),
+            (partner_hbm, partner),
+            (who_hbm, who_ref),
+            (mid_hbm, mid_ref),
+            (root_hbm, root_ref),
+            (leaf_hbm, leaf_ref),
+            (dev_hbm, dev_ref),
+            (group_hbm, group_ref),
         )
     ]
     for copy in copies:
         copy.start()
-    copies[0].wait()
-    copies[1].wait()
+    basis_copy.start()
+    for copy in copies:
+        copy.wait()
+    spread(leaf_scr, leaf_ref, 0, pitch_of(leaves), rank)
+    spread(scr, mid_ref, 0, 8, rank)
+    spread(scr, root_ref, middle, 8, rank)
+    spread(dev_scr, dev_ref, 0, pitch_of(slots), rank)
+    back_ref[...] = jnp.zeros_like(back_ref)
     stacked = jnp.concatenate(
         [vec_ref[:, h * SPLIT : (h + 1) * SPLIT].astype(bf16) for h in range(highs)], axis=0
     )
@@ -131,13 +135,7 @@
         for h in range(1, highs):
             picked = jnp.where(high == h, mixed[h * vecs : (h + 1) * vecs], picked)
         sorted_ref[:, k * step : (k + 1) * step] = picked
-    for copy in copies[2:]:
-        copy.wait()
-    spread(leaf_scr, leaf_ref, 0, pitch_of(leaves), rank)
-    spread(scr, mid_ref, 0, 8, rank)
-    spread(scr, root_ref, middle, 8, rank)
-    spread(dev_scr, dev_ref, 0, pitch_of(slots), rank)
-    back_ref[...] = jnp.zeros_like(back_ref)
+    basis_copy.wait()
     start = jnp.int32(0)
     coeffs = []
     for l in range(leaves):
@@ -210,7 +208,7 @@
             msg_ref[d] = tile
             msg_ref[d, :vecs, 2 * rank : 3 * rank] = back_ref[d].astype(bf16)
         some = pl.ds(8 * g, 8)
-        copies.append(pltpu.make_async_copy(msg_ref.at[some], msg_hbm.at[some], sems.at[g]))
+        copies.append(pltpu.make_async_copy(msg_ref.at[some], msg_hbm.at[some], sems.at[0]))
         copies[-1].start()
     for copy in copies:
         copy.wait()
@@ -231,7 +229,6 @@
     reach_ref,
     near_ref,
     dev_out,
-    root_out,
     leaf_scr,
     scr,
     dev_scr,
@@ -265,7 +262,6 @@
         wide_scr[jnp.where(who >= 0, who, subtrees), :, :rank] = block
     for b in range(subtrees):
         dev_out[:, 4 * rank * b : 4 * rank * (b + 1)] = wide_scr[b].astype(bf16)
-    root_out[...] = block_of(scr, middle, 8, rank)
     far_scr[...] = jnp.zeros_like(far_scr)
     for p in range(npairs):
         a = pairs[0, p]
@@ -300,14 +296,16 @@
         masked = jnp.concatenate([jnp.where(high == h, value, 0.0) for h in range(highs)], axis=0)
         result = result + dot(masked.astype(bf16), one_hot_low(morton, step), NT)
     for h in range(highs):
-        reach_ref[:, h * SPLIT : (h + 1) * SPLIT] = result[h * rows : h * rows + rank].astype(bf16)
+        reach = result[h * rows : h * rows + rank].astype(bf16)
+        reach_ref[:rank, h * SPLIT : (h + 1) * SPLIT] = reach
+        above = dot(block_of(scr, middle, 8, rank), reach, TN)
+        reach_ref[rank:, h * SPLIT : (h + 1) * SPLIT] = above.astype(bf16)
         near_ref[:, h * SPLIT : (h + 1) * SPLIT] = result[h * rows + rank : (h + 1) * rows]
 
 
 def last_kernel(
     got_ref,
     dev_ref,
-    root_ref,
     reach_ref,
     near_ref,
     out_hbm,
@@ -318,7 +316,7 @@
     *,
     few,
 ):
-    rank = root_ref.shape[0]
+    rank = dev_ref.shape[0]
     subtrees, tall, tile_lanes = got_ref.shape
     vecs = near_ref.shape[0]
     groups = subtrees // 8
@@ -358,14 +356,14 @@
             other = (own + 1 + q) % groups
             group = group_scr[other].astype(bf16)
             far = far + dot(group, stack_of(own, q), NT) + dot(group, stack_of(other, 0), NN)
-    total = (total + dot(far.astype(bf16), root_ref[...], NT)).astype(bf16)
+    total = beside([total, far]).astype(bf16)
     points = near_ref.shape[1]
-    pieces = sems.shape[0]
+    pieces = 4
     copies = []
     for n in range(pieces):
         cols = pl.ds(n * (points // pieces), points // pieces)
         out_ref[:, cols] = near_ref[:, cols] + dot(total, reach_ref[:, cols], NN)
-        copies.append(pltpu.make_async_copy(out_ref.at[:, cols], out_hbm.at[:, cols], sems.at[n]))
+        copies.append(pltpu.make_async_copy(out_ref.at[:, cols], out_hbm.at[:, cols], sems.at[0]))
         copies[-1].start()
     for copy in copies:
         copy.wait()
@@ -450,7 +448,7 @@
             )
         ]
         + [
-            pltpu.SemaphoreType.DMA((11,)),
+            pltpu.SemaphoreType.DMA((2,)),
             pltpu.VMEM((vecs, points), f32),
             pltpu.VMEM((rank * pitch_of(leaves), rank), f32),
             pltpu.VMEM((rank * 8, rank), f32),
@@ -484,22 +482,21 @@
             pltpu.VMEM((subtrees, tall, 4 * rank), bf16),
             pltpu.VMEM((rank * 2 * grp_coupling.shape[0], rank), f32),
             pltpu.VMEM((groups, rank // 2, rank), f32),
-            pltpu.SemaphoreType.DMA((groups,)),
+            pltpu.SemaphoreType.DMA((1,)),
         ],
         name="pack",
     )(keep(tops), keep(backs), *group_args)
     got = lax.all_to_all(message, "leaf", 0, 0, tiled=True)
 
-    reach, near, dev_wide, root_map = pl.pallas_call(
+    reach, near, dev_wide = pl.pallas_call(
         near_kernel,
         out_shape=(
-            made((rank, points), bf16),
+            made((2 * rank, points), bf16),
             made((vecs, points), f32),
             made((rank, subtrees * 4 * rank), bf16),
-            made((rank, rank), bf16),
         ),
         in_specs=[smem] * 3 + [vmem] * 8,
-        out_specs=(vmem,) * 4,
+        out_specs=(vmem,) * 3,
         scratch_shapes=[
             pltpu.VMEM((rank * pitch_of(leaves), rank), f32),
             pltpu.VMEM((rank * 8, rank), f32),
@@ -528,19 +525,18 @@
     return pl.pallas_call(
         functools.partial(last_kernel, few=few),
         out_shape=jax.ShapeDtypeStruct((vecs, points), f32),
-        in_specs=[vmem] * 5,
+        in_specs=[vmem] * 4,
         out_specs=pl.BlockSpec(memory_space=pl.ANY),
         scratch_shapes=[
             pltpu.VMEM((8 if few else subtrees * tall, 4 * rank), f32),
             pltpu.VMEM((groups, vecs, rank), f32),
             pltpu.VMEM((vecs, points), f32),
-            pltpu.SemaphoreType.DMA((4,)),
+            pltpu.SemaphoreType.DMA((1,)),
         ],
         name="last",
     )(
         keep(got),
         keep(dev_wide),
-        keep(root_map),
         keep(reach),
         keep(near),
     )

time: 22.2 us -> 22 us (level)
  no operation moved by 1% of the time
where the time goes in v4:
time: 22 us; the launch traced here: 21.8 us
  Pallas kernels  12.7 us (58%)
  starting transfers between devices  7.6 us (35%)
  waiting for transfers between devices  1.32 us (6%)
    pallas_call x1, Pallas kernels, body(): pl.pallas_call(near_kernel, out_shape=(made((2 * rank, points), bf16), ma...  7.81 us
    all_to_all x1, starting transfers between devices, body(): got = lax.all_to_all(message, 'leaf', 0, 0, tiled=True)  7.09 us
    pallas_call x1, Pallas kernels, body(): pl.pallas_call(up_kernel, out_shape=(made((leaves, vecs, rank), bf16), ma...  2.7 us
    all_to_all x1, waiting for transfers between devices, body(): got = lax.all_to_all(message, 'leaf', 0, 0, tiled=True)  1.32 us
    pallas_call x1, Pallas kernels, body(): pl.pallas_call(functools.partial(last_kernel, few=few), out_shape=jax.Sha...  1.23 us
    pallas_call x1, Pallas kernels, body(): pl.pallas_call(functools.partial(pack_kernel, few=few), out_shape=jax.Sha...  0.91 us
    ppermute x1, starting transfers between devices, body(): their_blocks = lax.ppermute(grp_coupling, 'leaf', swap)  0.49 us
  transfers between devices with their start and end apart: 3, of which 1 were waited for; matrix products, arithmetic and copies ran while one was open for 0% of the time, Pallas kernels for 48%

profile of v4, /device:TPU:1, one launch (start us, length us, event | category | flops | bytes accessed | tf_op | source)
XLA Modules:
  0.0 21.8 jit_solution(10617509609112416287)
XLA Ops:
  0.0 0.0 collective-permute-start
  0.0 0.5 %collective-permute-start.1 = (bf16[4,1024]{1,0:T(4,128)(2,1)}, bf16[4,1024]{1,0:T(4,128)(2,1)S(1)}, u32[]{:S(2)}, u32[]{:S(2)}) collective-permute-start(bf16[4,1024]{1,0:T(4,128)(2,1)} %group_hbm.1), channel_id=1, source_target_pairs={{0,1},{1,0},{2,3},{3,2},{4,5},{5,4},{6,7},{7,6},{8,9},{9,8},{10,11... | collective-permute-start | bytes 24584 | tf_op jit(solution)/shard_map/ppermute | solution.py:410
  0.5 2.7 %up.1 = (bf16[32,16,32]{2,1,0:T(8,128)(2,1)S(1)}, f32[16,64]{1,0:T(8,128)S(1)}, f32[32,16,32]{2,1,0:T(8,128)S(1)}, s32[1,4]{1,0:T(1,128)S(1)}, bf16[4,1024]{1,0:T(4,128)(2,1)S(1)}) custom-call(s32[1,32]{1,0:T(1,128)} %sizes.1, s32[1,16]{1,0:T(1,128)} %partner.1, f32[16,4096]{1,0:T(8,128)} %vec_hbm.1, s32[1,4096]{1,0:T(1,128)} %morton_ref.1, ...), custom_call_target="tpu_custom_call" | custom-call | flops 2147483648 | bytes 1048576 | tf_op jit(solution)/shard_map/up/pallas_call | solution.py:426
  3.2 0.0 collective-permute-done.rest_1_
  3.2 0.0 collective-permute-done.1.rest_3_
  3.2 0.0 copy-start.2
  3.3 0.0 copy-start.3
  3.3 0.0 copy-start.4
  3.3 0.0 copy-start.5
  3.3 0.0 copy-start.6
  3.3 0.9 %pack.1 = bf16[32,24,128]{2,1,0:T(8,128)(2,1)} custom-call(f32[16,64]{1,0:T(8,128)S(1)} %get-tuple-element.13.tops_ref, f32[32,16,32]{2,1,0:T(8,128)S(1)} %get-tuple-element.14.back_ref, s32[1,4]{1,0:T(1,128)S(1)} %get-tuple-element.15.rest_0_, s32[1,4]{1,0:T(1,128)S(1)} %collective-permute-done.rest_1_, bf16[4,1024]{1,0:T(4,128)(2,1)S(1)} %get-tuple-element.16.rest_2_, ...), custom_call_target="tpu_custom_call" | custom-call | tf_op jit(solution)/shard_map/pack/pallas_call | solution.py:476
  4.2 0.0 copy-start
  4.2 0.0 copy-start.1
  4.2 7.1 %all-to-all-start = ((bf16[32,24,128]{2,1,0:T(8,128)(2,1)}), bf16[32,24,128]{2,1,0:T(8,128)(2,1)S(1)}, u32[]{:S(2)}, u32[]{:S(2)}) async-start(bf16[32,24,128]{2,1,0:T(8,128)(2,1)} %pack.1), calls=%async_computation | async-start | bytes 393216 | tf_op jit(solution)/shard_map/all_to_all | solution.py:489
  11.3 0.0 copy-done.2
  11.3 0.0 copy-done.3
  11.4 0.0 copy-done.4
  11.4 0.0 copy-done.5
  11.4 0.0 copy-done.6
  11.4 0.0 copy-done
  11.4 0.0 copy-done.1
  11.4 7.8 %near.1 = (bf16[64,4096]{1,0:T(8,128)(2,1)S(1)}, f32[16,4096]{1,0:T(8,128)S(1)}, bf16[32,4096]{1,0:T(8,128)(2,1)S(1)}) custom-call(s32[1,32]{1,0:T(1,128)} %sizes.1, s32[2,64]{1,0:T(2,128)} %pairs.1, s32[1,16]{1,0:T(1,128)} %partner.1, bf16[32,16,32]{2,1,0:T(8,128)(2,1)S(1)} %get-tuple-element.17.coeff_ref, s32[1,4096]{1,0:T(1,128)S(1)} %copy-done.4, ...), custom_call_target="tpu_custom_call" | custom-call | flops 4294967296 | bytes 4194304 | tf_op jit(solution)/shard_map/near/pallas_call | solution.py:491
  19.2 1.3 %all-to-all-done.got_ref = bf16[32,24,128]{2,1,0:T(8,128)(2,1)S(1)} async-done(((bf16[32,24,128]{2,1,0:T(8,128)(2,1)}), bf16[32,24,128]{2,1,0:T(8,128)(2,1)S(1)}, u32[]{:S(2)}, u32[]{:S(2)}) %all-to-all-start) | async-done | bytes 196640 | tf_op jit(solution)/shard_map/all_to_all | solution.py:489
  20.5 1.2 %last.1 = f32[16,4096]{1,0:T(8,128)} custom-call(bf16[32,24,128]{2,1,0:T(8,128)(2,1)S(1)} %all-to-all-done.got_ref, bf16[32,4096]{1,0:T(8,128)(2,1)S(1)} %get-tuple-element.18.dev_ref, bf16[64,4096]{1,0:T(8,128)(2,1)S(1)} %get-tuple-element.19.reach_ref, f32[16,4096]{1,0:T(8,128)S(1)} %get-tuple-element.20.near_ref), custom_call_target="tpu_custom_call" | custom-call | tf_op jit(solution)/shard_map/last/pallas_call | solution.py:525
Async XLA Ops:
  0.0 3.2 %collective-permute-start = (s32[1,4]{1,0:T(1,128)}, s32[1,4]{1,0:T(1,128)S(1)}, u32[]{:S(2)}, u32[]{:S(2)}) collective-permute-start(s32[1,4]{1,0:T(1,128)} %who_hbm.1), channel_id=1, source_target_pairs={{0,1},{1,0},{2,3},{3,2},{4,5},{5,4},{6,7},{7,6},{8,9},{9,8},{10,11... | collective-permute-start | bytes 56 | tf_op jit(solution)/shard_map/ppermute | solution.py:409
  0.0 3.2 %collective-permute-start.1 = (bf16[4,1024]{1,0:T(4,128)(2,1)}, bf16[4,1024]{1,0:T(4,128)(2,1)S(1)}, u32[]{:S(2)}, u32[]{:S(2)}) collective-permute-start(bf16[4,1024]{1,0:T(4,128)(2,1)} %group_hbm.1), channel_id=1, source_target_pairs={{0,1},{1,0},{2,3},{3,2},{4,5},{5,4},{6,7},{7,6},{8,9},{9,8},{10,11... | collective-permute-start | bytes 24584 | tf_op jit(solution)/shard_map/ppermute | solution.py:410
  3.2 8.1 %copy-start.2 = (bf16[32,1024]{1,0:T(8,128)(2,1)S(1)}, bf16[32,1024]{1,0:T(8,128)(2,1)}, u32[]{:S(2)}) copy-start(bf16[32,1024]{1,0:T(8,128)(2,1)} %leaf_ref.1) | copy-start | bytes 196612
  3.3 8.1 %copy-start.3 = (bf16[16,1024]{1,0:T(8,128)(2,1)S(1)}, bf16[16,1024]{1,0:T(8,128)(2,1)}, u32[]{:S(2)}) copy-start(bf16[16,1024]{1,0:T(8,128)(2,1)} %dev_ref.1) | copy-start | bytes 98308
  3.3 8.1 %copy-start.4 = (s32[1,4096]{1,0:T(1,128)S(1)}, s32[1,4096]{1,0:T(1,128)}, u32[]{:S(2)}) copy-start(s32[1,4096]{1,0:T(1,128)} %morton_ref.1) | copy-start | bytes 49156
  3.3 8.1 %copy-start.5 = (bf16[4,1024]{1,0:T(4,128)(2,1)S(1)}, bf16[4,1024]{1,0:T(4,128)(2,1)}, u32[]{:S(2)}) copy-start(bf16[4,1024]{1,0:T(4,128)(2,1)} %mid_ref.1) | copy-start | bytes 24580
  3.3 8.1 %copy-start.6 = (bf16[1,1024]{1,0:T(2,128)(2,1)S(1)}, bf16[1,1024]{1,0:T(2,128)(2,1)}, u32[]{:S(2)}) copy-start(bf16[1,1024]{1,0:T(2,128)(2,1)} %root_ref.1) | copy-start | bytes 6148
  4.2 7.2 %copy-start = (bf16[32,4096]{1,0:T(8,128)(2,1)S(1)}, bf16[32,4096]{1,0:T(8,128)(2,1)}, u32[]{:S(2)}) copy-start(bf16[32,4096]{1,0:T(8,128)(2,1)} %basis_ref.1) | copy-start | bytes 786436
  4.2 7.2 %copy-start.1 = (bf16[64,1024]{1,0:T(8,128)(2,1)S(1)}, bf16[64,1024]{1,0:T(8,128)(2,1)}, u32[]{:S(2)}) copy-start(bf16[64,1024]{1,0:T(8,128)(2,1)} %couple_ref.1) | copy-start | bytes 393220
  4.2 16.3 %all-to-all-start = ((bf16[32,24,128]{2,1,0:T(8,128)(2,1)}), bf16[32,24,128]{2,1,0:T(8,128)(2,1)S(1)}, u32[]{:S(2)}, u32[]{:S(2)}) async-start(bf16[32,24,128]{2,1,0:T(8,128)(2,1)} %pack.1), calls=%async_computation | async-start | bytes 393216 | tf_op jit(solution)/shard_map/all_to_all | solution.py:489
